TPU v7x, 256 devices: a whole 4x4x8 slice. The times are simulated.
256 devices in a mesh: row: 16 (over x, y), col: 8 (over z), depth: 2 (over core).
Axes of the slice: x: 4, y: 4, z: 8, core: 2. Of those that a mesh axis runs over, the one named last changes fastest.
Arguments:
- covariance: float32 [3, 16, 6, 8, 256, 256], P(None, 'row', None, 'col'), may hold values from 0 to 2, as said below
Outputs:
- factored: float32 [3, 16, 6, 8, 256, 256], P(None, 'row', None, 'col', 'depth')
Inputs may be any that keep to these rules, and one draw needn't show every extreme that they name: covariance is the Matern kernel of smoothness 3/2, (1 + rho) exp(-rho) with rho = sqrt(3) times the scaled distance, over 12288 points in the unit cube of 8 coordinates with length scales between 0.3 and 1.2, plus a nugget between 0.2 and 1 on the diagonal; it is symmetric positive definite.
All inputs are finite; a program needn't handle non-finite values.
Results may differ from a plain program's by a relative error of at most 0.0003.
Values sent between devices are 32-bit elements; how exact they have to be, the bound alone decides.
A program may use at most 128 MiB of HBM per device.

v0:
```python
import functools

import jax
import jax.numpy as jnp
from jax import lax
from jax.experimental import pallas as pl
from jax.experimental.pallas import tpu as pltpu
from jax.sharding import PartitionSpec as P

TILE = 256
PANEL = 512
NB = 128
NX = NY = 4
NZ = 8
DCH = 32
CCH = 64
MESH = pl.DeviceIdType.MESH
HIGHEST = lax.Precision.HIGHEST
F32 = jnp.float32
BF16 = jnp.bfloat16


def dot_nt(a, b):
    dims = (((1,), (1,)), ((), ()))
    return lax.dot_general(a, b, dims, precision=HIGHEST, preferred_element_type=F32)


def dot_nn(a, b):
    dims = (((1,), (0,)), ((), ()))
    return lax.dot_general(a, b, dims, precision=HIGHEST, preferred_element_type=F32)


def split(x):
    hi = x.astype(BF16)
    return hi, (x - hi.astype(F32)).astype(BF16)


def dot3(a, b, dims):
    (ah, al), (bh, bl) = a, b
    dot = functools.partial(lax.dot_general, dimension_numbers=(dims, ((), ())), preferred_element_type=F32)
    return dot(ah, bh) + (dot(ah, bl) + dot(al, bh))


def lane_copy(v, k):
    return jnp.broadcast_to(v[:, k : k + 1], (8, NB))


def row_copy(v, k):
    return jnp.broadcast_to(v[k : k + 1, :], (8, NB))


def inverse_factor(rows):
    rows = list(rows)
    lane = lax.broadcasted_iota(jnp.int32, (8, NB), 1)
    sub = lax.broadcasted_iota(jnp.int32, (8, NB), 0)
    out = []
    for b in range(16):
        base = 8 * b
        cols = [[lane_copy(rows[i], base + k) for k in range(8)] for i in range(b, 16)]
        inside = (lane >= base) & (lane < base + 8)
        cur = jnp.where(inside, jnp.where(lane == sub + base, 1.0, 0.0), rows[b])
        diag = cols[0]
        scaled = jnp.zeros((8, NB), F32)
        for k in range(8):
            d = row_copy(diag[k], k)
            r = 1.0 / d
            scaled = jnp.where(sub == k, cur * lax.rsqrt(d), scaled)
            less = jnp.where(sub == k, diag[k] - 1.0, diag[k])
            for j in range(k + 1, 8):
                diag[j] = diag[j] - less * (row_copy(diag[k], j) * r)
            cur = cur - less * (row_copy(cur, k) * r)
        for i in range(b + 1, 16):
            acc = jnp.where(inside, 0.0, rows[i])
            for j in range(8):
                acc = acc - cols[i - b][j] * row_copy(cur, j)
            rows[i] = acc
        out.append(jnp.where(lane < base + 8, scaled, 0.0))
    return out


def gather_kernel(
    cov, pct_out, rp_out, w_out, pct, rp, s, w,
    d_recv, c_recv, r_recv, w_recv, d_core, c_core, r_core,
    d_send, c_send, r_send, k_send, w_send, out_sem,
):
    row = lax.axis_index("row")
    z = lax.axis_index("col")
    core = lax.axis_index("depth")
    x, y = row // NY, row % NY

    def at(xx, yy, zz):
        return {"row": lax.rem(xx + NX, NX) * NY + lax.rem(yy + NY, NY), "col": lax.rem(zz + NZ, NZ), "depth": 1}

    links = [at(x + 1, y, z), at(x - 1, y, z), at(x, y + 1, z), at(x, y - 1, z), at(x, y, z + 1), at(x, y, z - 1)]
    partner = {"row": row, "col": z, "depth": 1 - core}

    barrier = pltpu.get_barrier_semaphore()
    pl.semaphore_signal(barrier, inc=1, device_id=partner, device_id_type=MESH)

    @pl.when(core == 1)
    def _():
        for link in links:
            pl.semaphore_signal(barrier, inc=1, device_id=link, device_id_type=MESH)
        pl.semaphore_wait(barrier, 7)

    @pl.when(core == 0)
    def _():
        pl.semaphore_wait(barrier, 1)

    def remote(src, dst, send, recv, to):
        return pltpu.make_async_remote_copy(src, dst, send, recv, device_id=to, device_id_type=MESH)

    tiles = ((0, 0, 0, 0), (1, 0, 1, 0), (1, 1, 1, 1))
    per_tile = TILE // DCH

    def d_rows(t, i):
        _, _, ti, tj = tiles[t]
        return s.at[pl.ds(ti * TILE + i * DCH, DCH), pl.ds(tj * TILE, TILE)]

    def d_children(t):
        src_row, src_z, _, _ = tiles[t]
        dx, dy, dz = x, lax.rem(y - src_row + NY, NY), lax.rem(z - src_z + NZ, NZ)
        line = (dx == 0) & (dy == 0)
        return [
            (0, (dy == 0) & (dx <= 1)),
            (1, (dy == 0) & (dx == 0)),
            (2, dy <= 1),
            (3, dy == 0),
            (4, line & (dz <= 3)),
            (5, line & ((dz == 0) | (dz >= 6))),
        ], line & (dz == 0)

    def c_children(src, q):
        dx, dy = x, lax.rem(y - src + NY, NY)
        if q == 0:
            kids = [(0, (dy == 0) & (dx <= 2)), (2, dy <= 2)]
        elif q == 1:
            kids = [(1, (dy == 0) & (dx != 1)), (3, dy != 1)]
        elif q == 2:
            kids = [(2, (dx == 0) & (dy <= 2)), (0, dx <= 2)]
        else:
            kids = [(3, (dx == 0) & (dy != 1)), (1, dx != 1)]
        return kids, (dx == 0) & (dy == 0)

    def r_child(c, way):
        if way == 0:
            dz = lax.rem(z - c + NZ, NZ)
            return 4, dz <= 6, dz == 0
        dz = lax.rem(c - z + NZ, NZ)
        return 5, dz <= 6, dz == 0

    def pass_on(src, dst, here, arrived, kids, sends, recv, to_core):
        @pl.when(jnp.logical_not(here))
        def _():
            remote(dst, dst, sends(0), recv, partner).wait_recv()
        @pl.when(here)
        def _():
            for n, (link, cond) in enumerate(kids):
                @pl.when(cond)
                def _():
                    remote(src, dst, sends(n), recv, links[link]).start()
            to_core(src)
        @pl.when(jnp.logical_not(here))
        def _():
            for n, (link, cond) in enumerate(kids):
                @pl.when(cond)
                def _():
                    remote(dst, dst, sends(n), recv, links[link]).start()
            to_core(dst)

    @pl.when(core == 1)
    def _():
        for t in range(3):
            kids, here = d_children(t)
            @pl.loop(0, per_tile)
            def _(i):
                dst = d_rows(t, i)
                src = cov.at[0, 0, 0, 0, pl.ds(i * DCH, DCH), :]
                def to_core(ref):
                    remote(ref, dst, k_send.at[0, t], d_core.at[t, i], partner).start()
                pass_on(src, dst, here, None, kids, lambda n: d_send.at[t, n], d_recv.at[t, i], to_core)

        @pl.loop(0, 6)
        def _(b):
            for q in range(4):
                for src_row in range(2):
                    kids, here = c_children(src_row, q)
                    src = cov.at[0, 0, b, 0, pl.ds(q * CCH, CCH), :]
                    dst = pct.at[src_row, b, pl.ds(q * CCH, CCH), :]
                    def to_core(ref):
                        remote(ref, dst, k_send.at[1, src_row * 4 + q], c_core.at[src_row, q, b], partner).start()
                    pass_on(src, dst, here, None, kids, lambda n: c_send.at[src_row, q, n], c_recv.at[src_row, q, b], to_core)
            a, sub = b // 2, b % 2
            for way in range(2):
                for c in range(2):
                    link, cond, here = r_child(c, way)
                    rows = pl.ds(way * NB + sub * CCH, CCH)
                    src = cov.at[a, 0, 0, 0, rows, :]
                    dst = rp.at[c, a, rows, :]
                    def to_core(ref):
                        if way == 0:
                            remote(ref, dst, k_send.at[2, c], r_core.at[c, b], partner).start()
                    pass_on(src, dst, here, None, [(link, cond)], lambda n: r_send.at[c, way], r_recv.at[c, way, b], to_core)

        @pl.when((x == 0) & (y <= 1))
        def _():
            copy = pltpu.make_async_copy(cov.at[0, 0, :, 0], pct.at[y], out_sem.at[0])
            copy.start()
            copy.wait()
        @pl.when(z <= 1)
        def _():
            copy = pltpu.make_async_copy(cov.at[:, 0, 0, 0], rp.at[z], out_sem.at[0])
            copy.start()
            copy.wait()

        for t in range(3):
            kids, _ = d_children(t)
            _, _, ti, tj = tiles[t]
            whole = s.at[pl.ds(ti * TILE, TILE), pl.ds(tj * TILE, TILE)]
            for n, (link, cond) in enumerate(kids):
                @pl.when(cond)
                def _():
                    remote(whole, whole, d_send.at[t, n], d_recv.at[t, 0], partner).wait_send()
            remote(whole, whole, k_send.at[0, t], d_recv.at[t, 0], partner).wait_send()
        for src_row in range(2):
            for q in range(4):
                kids, _ = c_children(src_row, q)
                whole = pct.at[src_row, :, pl.ds(q * CCH, CCH), :]
                for n, (link, cond) in enumerate(kids):
                    @pl.when(cond)
                    def _():
                        remote(whole, whole, c_send.at[src_row, q, n], d_recv.at[0, 0], partner).wait_send()
                remote(whole, whole, k_send.at[1, src_row * 4 + q], d_recv.at[0, 0], partner).wait_send()
        for c in range(2):
            for way in range(2):
                _, cond, _ = r_child(c, way)
                whole = rp.at[c, :, pl.ds(way * NB, NB), :]
                @pl.when(cond)
                def _():
                    remote(whole, whole, r_send.at[c, way], d_recv.at[0, 0], partner).wait_send()
                if way == 0:
                    remote(whole, whole, k_send.at[2, c], d_recv.at[0, 0], partner).wait_send()
        for k in range(4):
            rows = w.at[pl.ds(k * NB, NB), :]
            remote(rows, rows, w_send.at[k], w_recv.at[k], partner).wait_recv()

    @pl.when(core == 0)
    def _():
        def wait_d(t, lo, hi):
            @pl.loop(lo, hi)
            def _(i):
                dst = d_rows(t, i)
                remote(dst, dst, d_send.at[t, 0], d_core.at[t, i], partner).wait_recv()

        w[...] = jnp.zeros_like(w)
        for k in range(4):
            o = k * NB
            e = o + NB
            if k == 0:
                wait_d(0, 0, NB // DCH)
            wk = jnp.concatenate(inverse_factor([s[o + 8 * i : o + 8 * i + 8, o:e] for i in range(16)]), axis=0)
            if k > 0:
                w[o:e, :o] = dot_nn(wk, w[o:e, :o])
            w[o:e, o:e] = wk
            rows = w.at[pl.ds(o, NB), :]
            remote(rows, rows, w_send.at[k], w_recv.at[k], partner).start()
            if k == 0:
                wait_d(0, NB // DCH, per_tile)
                wait_d(1, 0, per_tile)
                wait_d(2, 0, per_tile)
            if k < 3:
                low = dot_nt(s[e:, o:e], wk)
                for j in range(k + 1, 4):
                    f = j * NB
                    s[f:, f : f + NB] = s[f:, f : f + NB] - dot_nt(low[f - e :], low[f - e : f - e + NB])
                w[e:, :e] = w[e:, :e] - dot_nn(low, w[o:e, :e])

        @pl.loop(0, 6)
        def _(b):
            for q in range(4):
                for src_row in range(2):
                    dst = pct.at[src_row, b, pl.ds(q * CCH, CCH), :]
                    remote(dst, dst, d_send.at[0, 0], c_core.at[src_row, q, b], partner).wait_recv()
            a, sub = b // 2, b % 2
            for c in range(2):
                dst = rp.at[c, a, pl.ds(sub * CCH, CCH), :]
                remote(dst, dst, d_send.at[0, 0], r_core.at[c, b], partner).wait_recv()
        for k in range(4):
            rows = w.at[pl.ds(k * NB, NB), :]
            remote(rows, rows, w_send.at[k], w_recv.at[k], partner).wait_send()

    copies = [
        pltpu.make_async_copy(pct, pct_out, out_sem.at[0]),
        pltpu.make_async_copy(rp.at[:, :, pl.ds(core * NB, NB), :], rp_out, out_sem.at[1]),
        pltpu.make_async_copy(w, w_out, out_sem.at[2]),
    ]
    for copy in copies:
        copy.start()
    for copy in copies:
        copy.wait()


def gather(cov):
    dma = pltpu.SemaphoreType.DMA
    per_tile = TILE // DCH
    return pl.pallas_call(
        gather_kernel,
        out_shape=(
            jax.ShapeDtypeStruct((2, 6, TILE, TILE), F32),
            jax.ShapeDtypeStruct((2, 3, NB, TILE), F32),
            jax.ShapeDtypeStruct((PANEL, PANEL), F32),
        ),
        in_specs=[pl.BlockSpec(memory_space=pl.ANY)],
        out_specs=[pl.BlockSpec(memory_space=pl.ANY)] * 3,
        scratch_shapes=[
            pltpu.VMEM((2, 6, TILE, TILE), F32),
            pltpu.VMEM((2, 3, TILE, TILE), F32),
            pltpu.VMEM((PANEL, PANEL), F32),
            pltpu.VMEM((PANEL, PANEL), F32),
            dma((3, per_tile)), dma((2, 4, 6)), dma((2, 2, 6)), dma((4,)),
            dma((3, per_tile)), dma((2, 4, 6)), dma((2, 6)),
            dma((3, 6)), dma((2, 4, 2)), dma((2, 2)), dma((3, 8)), dma((4,)), dma((3,)),
        ],
        compiler_params=pltpu.CompilerParams(collective_id=0, has_side_effects=True),
        name="gather_and_factor",
    )(cov)


def update_kernel(where, cov, pct, rp, w, out, c_all, t_hi, t_lo):
    b = pl.program_id(0)
    row, z, core = where[0], where[1], where[2]
    nt, nn = ((1,), (1,)), ((1,), (0,))

    @pl.when(b == 0)
    def _():
        wsplit = split(w[...])
        rows = jnp.concatenate([rp[c].reshape(3 * NB, TILE) for c in range(2)], axis=1)
        c = dot3(split(rows), wsplit, nt)
        c_all[...] = c
        hi, lo = split(dot3(split(c), wsplit, nn))
        t_hi[...] = hi
        t_lo[...] = lo

    cols = jnp.concatenate([pct[0, 0], pct[1, 0]], axis=0)
    old = cov[:, 0, 0, 0].reshape(3 * NB, TILE)
    new = old - dot3((t_hi[...], t_lo[...]), split(cols), nn)
    sub = lax.broadcasted_iota(jnp.int32, (3 * NB, TILE), 0)
    lane = lax.broadcasted_iota(jnp.int32, (3 * NB, TILE), 1)
    top = (sub < NB) & (row < 2)
    out[...] = jnp.where(top, 0.0, new).reshape(3, 1, 1, 1, NB, TILE)

    @pl.when((b == 0) & (z < 2))
    def _():
        mine = jnp.where(z == 0, c_all[:, :TILE], c_all[:, TILE:])
        above = top & (row * TILE + core * NB + sub < z * TILE + lane)
        out[...] = jnp.where(above, 0.0, mine).reshape(3, 1, 1, 1, NB, TILE)


def update(where, cov, pct, rp, w):
    grid_spec = pltpu.PrefetchScalarGridSpec(
        num_scalar_prefetch=1,
        grid=(6,),
        in_specs=[
            pl.BlockSpec((3, 1, 1, 1, NB, TILE), lambda b, p: (0, 0, b, 0, p[2], 0)),
            pl.BlockSpec((2, 1, TILE, TILE), lambda b, p: (0, b, 0, 0)),
            pl.BlockSpec((2, 3, NB, TILE), lambda b, p: (0, 0, 0, 0)),
            pl.BlockSpec((PANEL, PANEL), lambda b, p: (0, 0)),
        ],
        out_specs=pl.BlockSpec((3, 1, 1, 1, NB, TILE), lambda b, p: (0, 0, b, 0, 0, 0)),
        scratch_shapes=[
            pltpu.VMEM((3 * NB, PANEL), F32),
            pltpu.VMEM((3 * NB, PANEL), BF16),
            pltpu.VMEM((3 * NB, PANEL), BF16),
        ],
    )
    return pl.pallas_call(
        update_kernel,
        out_shape=jax.ShapeDtypeStruct((3, 1, 6, 1, NB, TILE), F32),
        grid_spec=grid_spec,
        name="update",
    )(where, cov, pct, rp, w)


def on_device(covariance):
    where = jnp.stack([lax.axis_index("row"), lax.axis_index("col"), lax.axis_index("depth")])
    pct, rp, w = gather(covariance)
    return update(where, covariance, pct, rp, w)


def solution(mesh):
    return jax.shard_map(
        on_device,
        mesh=mesh,
        in_specs=(P(None, "row", None, "col", None, None),),
        out_specs=P(None, "row", None, "col", "depth", None),
        check_vma=False,
    )
```

profile of v0, /device:TPU:83, one launch (start us, length us, event | category | flops | bytes accessed | tf_op | source)
XLA Modules:
  0.0 630.3 jit_solution(2321628342226987743)
XLA Ops:
  0.0 0.6 pad_add_fusion.where
  0.6 620.2 %gather_and_factor.1 = (f32[2,6,256,256]{3,2,1,0:T(8,128)}, f32[2,3,128,256]{3,2,1,0:T(8,128)}, f32[512,512]{1,0:T(8,128)}) custom-call(f32[3,1,6,1,256,256]{5,4,3,2,1,0:T(8,128)} %cov.3), custom_call_target="tpu_custom_call" | custom-call | tf_op jit(solution)/shard_map/gather_and_factor/pallas_call | solution.py:306
  620.8 9.5 %update.1 = f32[3,1,6,1,128,256]{5,4,3,2,1,0:T(8,128)} custom-call(s32[3]{0:T(128)} %pad_add_fusion.where, f32[3,1,6,1,256,256]{5,4,3,2,1,0:T(8,128)} %cov.3, f32[2,6,256,256]{3,2,1,0:T(8,128)} %get-tuple-element.8.pct, f32[2,3,128,256]{3,2,1,0:T(8,128)} %get-tuple-element.9.rp, f32[512,512]{1,0:T(8,128)} %get-tuple-element.10.w), custom_call_target="tpu_custom_call" | custom-call | tf_op jit(solution)/shard_map/update/pallas_call | solution.py:376
where the time goes:
time: 631 us; the launch traced here: 630 us
  Pallas kernels  630 us (100%)
    pallas_call x1, Pallas kernels, gather(): pl.pallas_call(gather_kernel, out_shape=(jax.ShapeDtypeStruct((2, 6, TILE...  620 us

commit v1 on v0

v1 whole, which is shorter than its diff:
```python
import functools

import jax
import jax.numpy as jnp
from jax import lax
from jax.experimental import pallas as pl
from jax.experimental.pallas import tpu as pltpu
from jax.sharding import PartitionSpec as P

TILE = 256
PANEL = 512
NB = 128
NX = NY = 4
NZ = 8
CCH = 32
TURNS = 6 * (TILE // 4 // CCH) + 2 * 7
MESH = pl.DeviceIdType.MESH
HIGHEST = lax.Precision.HIGHEST
F32 = jnp.float32
BF16 = jnp.bfloat16


def dot_nt(a, b):
    dims = (((1,), (1,)), ((), ()))
    return lax.dot_general(a, b, dims, precision=HIGHEST, preferred_element_type=F32)


def dot_nn(a, b):
    dims = (((1,), (0,)), ((), ()))
    return lax.dot_general(a, b, dims, precision=HIGHEST, preferred_element_type=F32)


def split(x):
    hi = x.astype(BF16)
    return hi, (x - hi.astype(F32)).astype(BF16)


def dot3(a, b, dims):
    (ah, al), (bh, bl) = a, b
    dot = functools.partial(lax.dot_general, dimension_numbers=(dims, ((), ())), preferred_element_type=F32)
    return dot(ah, bh) + (dot(ah, bl) + dot(al, bh))


def lane_copy(v, k):
    return jnp.broadcast_to(v[:, k : k + 1], (8, NB))


def row_copy(v, k):
    return jnp.broadcast_to(v[k : k + 1, :], (8, NB))


def inverse_factor(rows):
    rows = list(rows)
    lane = lax.broadcasted_iota(jnp.int32, (8, NB), 1)
    sub = lax.broadcasted_iota(jnp.int32, (8, NB), 0)
    out = []
    for b in range(16):
        base = 8 * b
        cols = [[lane_copy(rows[i], base + k) for k in range(8)] for i in range(b, 16)]
        inside = (lane >= base) & (lane < base + 8)
        cur = jnp.where(inside, jnp.where(lane == sub + base, 1.0, 0.0), rows[b])
        diag = cols[0]
        scaled = jnp.zeros((8, NB), F32)
        for k in range(8):
            d = row_copy(diag[k], k)
            r = 1.0 / d
            scaled = jnp.where(sub == k, cur * lax.rsqrt(d), scaled)
            less = jnp.where(sub == k, diag[k] - 1.0, diag[k])
            for j in range(k + 1, 8):
                diag[j] = diag[j] - less * (row_copy(diag[k], j) * r)
            cur = cur - less * (row_copy(cur, k) * r)
        for i in range(b + 1, 16):
            acc = jnp.where(inside, 0.0, rows[i])
            for j in range(8):
                acc = acc - cols[i - b][j] * row_copy(cur, j)
            rows[i] = acc
        out.append(jnp.where(lane < base + 8, scaled, 0.0))
    return out


def gather_kernel(
    cov, pct_out, rp_out, w_out, pct, rp, s, w,
    b_recv, d_recv, c_recv, r_recv, w_recv, d_core, c_core, r_core,
    b_send, d_send, c_send, r_send, k_send, w_send, out_sem,
):
    row = lax.axis_index("row")
    z = lax.axis_index("col")
    core = lax.axis_index("depth")
    x, y = row // NY, row % NY

    def at(xx, yy, zz, cc):
        return {"row": lax.rem(xx + NX, NX) * NY + lax.rem(yy + NY, NY), "col": lax.rem(zz + NZ, NZ), "depth": cc}

    def remote(src, dst, send, recv, to):
        return pltpu.make_async_remote_copy(src, dst, send, recv, device_id=to, device_id_type=MESH)

    partner = {"row": row, "col": z, "depth": 1 - core}
    links = [
        at(x + 1, y, z, 1), at(x - 1, y, z, 1), at(x, y + 1, z, 1),
        at(x, y - 1, z, 1), at(x, y, z + 1, 1), at(x, y, z - 1, 1),
    ]
    on_z = (row == 0) & (z == 0)
    on_y = row == 0
    on_x = x == 0
    z_kids = [at(x, y, z + n, 0) for n in (4, 5, 3, 6, 2, 7, 1)]
    y_kids = [at(x, y + n, z, 0) for n in (2, 1, 3)]
    x_kids = [at(x + n, y, z, 0) for n in (2, 1, 3)]
    trees = [(on_z, z_kids), (on_y, y_kids), (on_x, x_kids)]

    barrier = pltpu.get_barrier_semaphore()
    pl.semaphore_signal(barrier, inc=1, device_id=partner, device_id_type=MESH)

    @pl.when(core == 1)
    def _():
        for link in links:
            pl.semaphore_signal(barrier, inc=1, device_id=link, device_id_type=MESH)
        pl.semaphore_wait(barrier, 7)

    @pl.when(core == 0)
    def _():
        @pl.when(jnp.logical_not(on_x))
        def _():
            pl.semaphore_signal(barrier, inc=1, device_id=at(0 * x, y, z, 0), device_id_type=MESH)
        @pl.when(on_x & jnp.logical_not(on_y))
        def _():
            pl.semaphore_signal(barrier, inc=1, device_id=at(x, 0 * y, z, 0), device_id_type=MESH)
        @pl.when(on_y & (z != 0))
        def _():
            pl.semaphore_signal(barrier, inc=1, device_id=at(x, y, 0 * z, 0), device_id_type=MESH)
        pl.semaphore_wait(barrier, 1 + sum(cond.astype(jnp.int32) * len(kids) for cond, kids in trees))

    blocks = [(i, j) for i in range(1, 4) for j in range(i + 1)]

    def d_place(n):
        i, j = blocks[n]
        return s.at[pl.ds(i * NB, NB), pl.ds(j * NB, NB)]

    def d_tree(n):
        i, j = blocks[n]
        src_row, src_z = i // 2, j // 2
        dx, dy, dz = x, lax.rem(y - src_row + NY, NY), lax.rem(z - src_z + NZ, NZ)
        line = (dx == 0) & (dy == 0)
        kids = [
            (4, line & (dz <= 3)),
            (5, line & ((dz == 0) | (dz >= 6))),
            (0, (dy == 0) & (dx <= 1)),
            (1, (dy == 0) & (dx == 0)),
            (2, dy <= 1),
            (3, dy == 0),
        ]
        hops = jnp.minimum(dz, NZ - dz) + jnp.minimum(dx, NX - dx) + jnp.minimum(dy, NY - dy)
        return kids, line & (dz == 0), hops

    def c_tree(src, q):
        dx, dy = x, lax.rem(y - src + NY, NY)
        bx, by = lax.rem(NX - dx, NX), lax.rem(NY - dy, NY)
        if q == 0:
            return [(0, (dy == 0) & (dx <= 2)), (2, dy <= 2)], dx + dy
        if q == 1:
            return [(1, (dy == 0) & (bx <= 2)), (3, by <= 2)], bx + by
        if q == 2:
            return [(2, (dx == 0) & (dy <= 2)), (0, dx <= 2)], dx + dy
        return [(3, (dx == 0) & (by <= 2)), (1, bx <= 2)], bx + by

    def r_tree(c, way):
        hops = lax.rem((z - c if way == 0 else c - z) + NZ, NZ)
        return [(4 + way, hops <= 6)], hops

    def pass_on(live, src, dst, here, kids, sends, recv, to_core):
        def forward(ref):
            for n, (link, cond) in enumerate(kids):
                @pl.when(cond)
                def _():
                    remote(ref, dst, sends(n), recv, links[link]).start()
            to_core(ref)

        @pl.when(live & here)
        def _():
            forward(src)

        @pl.when(live & jnp.logical_not(here))
        def _():
            remote(dst, dst, sends(0), recv, partner).wait_recv()
            forward(dst)

    n_c = TILE // 4 // CCH * 6
    n_r = NB // CCH * 3

    @pl.when(core == 1)
    def _():
        @pl.loop(0, TURNS)
        def _(g):
            for n, (bi, bj) in enumerate(blocks):
                kids, here, hops = d_tree(n)
                src = cov.at[0, 0, 0, 0, pl.ds(bi % 2 * NB, NB), pl.ds(bj % 2 * NB, NB)]
                dst = d_place(n)
                def to_core(ref):
                    remote(ref, dst, k_send.at[0, n], d_core.at[n], partner).start()
                pass_on(g == n // 2 + 2 * hops, src, dst, here, kids, lambda m: d_send.at[n, m], d_recv.at[n], to_core)
            for q in range(4):
                for src_row in range(2):
                    kids, hops = c_tree(src_row, q)
                    i = g - 2 * hops
                    live = (i >= 0) & (i < n_c)
                    i = jnp.clip(i, 0, n_c - 1)
                    per = n_c // 6
                    b = i // per
                    rows = pl.ds(pl.multiple_of(q * (TILE // 4) + i % per * CCH, CCH), CCH)
                    src = cov.at[0, 0, b, 0, rows, :]
                    dst = pct.at[src_row, b, rows, :]
                    def to_core(ref):
                        remote(ref, dst, k_send.at[1, src_row * 4 + q], c_core.at[src_row, q, i], partner).start()
                    pass_on(live, src, dst, hops == 0, kids, lambda m: c_send.at[src_row, q, m], c_recv.at[src_row, q, i], to_core)
            for way in range(2):
                for c in range(2):
                    kids, hops = r_tree(c, way)
                    i = g - 2 * hops
                    live = (i >= 0) & (i < n_r)
                    i = jnp.clip(i, 0, n_r - 1)
                    per = n_r // 3
                    a = i // per
                    rows = pl.ds(pl.multiple_of(way * NB + i % per * CCH, CCH), CCH)
                    src = cov.at[a, 0, 0, 0, rows, :]
                    dst = rp.at[c, a, rows, :]
                    def to_core(ref):
                        if way == 0:
                            remote(ref, dst, k_send.at[2, c], r_core.at[c, i], partner).start()
                    pass_on(live, src, dst, hops == 0, kids, lambda m: r_send.at[c, way], r_recv.at[c, way, i], to_core)

        @pl.when((x == 0) & (y <= 1))
        def _():
            copy = pltpu.make_async_copy(cov.at[0, 0, :, 0], pct.at[y], out_sem.at[0])
            copy.start()
            copy.wait()
        @pl.when(z <= 1)
        def _():
            copy = pltpu.make_async_copy(cov.at[:, 0, 0, 0], rp.at[z], out_sem.at[0])
            copy.start()
            copy.wait()

        def left(whole, send):
            remote(whole, whole, send, d_recv.at[0], partner).wait_send()
        for n in range(len(blocks)):
            kids, _, _ = d_tree(n)
            for m, (_, cond) in enumerate(kids):
                @pl.when(cond)
                def _():
                    left(d_place(n), d_send.at[n, m])
            left(d_place(n), k_send.at[0, n])
        for src_row in range(2):
            for q in range(4):
                kids, _ = c_tree(src_row, q)
                whole = pct.at[src_row, :, pl.ds(q * (TILE // 4), TILE // 4), :]
                for m, (_, cond) in enumerate(kids):
                    @pl.when(cond)
                    def _():
                        left(whole, c_send.at[src_row, q, m])
                left(whole, k_send.at[1, src_row * 4 + q])
        for c in range(2):
            for way in range(2):
                kids, _ = r_tree(c, way)
                whole = rp.at[c, :, pl.ds(way * NB, NB), :]
                @pl.when(kids[0][1])
                def _():
                    left(whole, r_send.at[c, way])
                if way == 0:
                    left(whole, k_send.at[2, c])
        for k in range(4):
            rows = w.at[pl.ds(k * NB, NB), :]
            remote(rows, rows, w_send.at[k], w_recv.at[k], partner).wait_recv()

    @pl.when(core == 0)
    def _():
        first = s.at[pl.ds(0, NB), pl.ds(0, NB)]

        @pl.when(on_z)
        def _():
            copy = pltpu.make_async_copy(cov.at[0, 0, 0, 0, pl.ds(0, NB), pl.ds(0, NB)], first, out_sem.at[0])
            copy.start()
            copy.wait()
        @pl.when(jnp.logical_not(on_z))
        def _():
            remote(first, first, b_send.at[0], b_recv, partner).wait_recv()
        slot = 0
        for cond, kids in trees:
            @pl.when(cond)
            def _():
                for n, kid in enumerate(kids):
                    remote(first, first, b_send.at[slot + n], b_recv, kid).start()
            slot += len(kids)

        def block(i, j):
            return s[i * NB : (i + 1) * NB, j * NB : (j + 1) * NB]

        def wait_row(i):
            for n, at_n in enumerate(blocks):
                if at_n[0] == i:
                    remote(d_place(n), d_place(n), b_send.at[0], d_core.at[n], partner).wait_recv()

        w[...] = jnp.zeros_like(w)
        low = {}
        inv = {}
        for k in range(4):
            o = k * NB
            e = o + NB
            piv = block(k, k)
            if k > 0:
                low[k, k - 1] = dot_nt(low.pop((k, "left")), inv[k - 1])
                for j in range(k):
                    piv = piv - dot_nt(low[k, j], low[k, j])
                lk = jnp.concatenate([low[k, j] for j in range(k)], axis=1)
                mk = dot_nn(lk, w[:o, :o])
            wk = jnp.concatenate(inverse_factor([piv[8 * i : 8 * i + 8] for i in range(16)]), axis=0)
            inv[k] = wk
            if k > 0:
                w[o:e, :o] = -dot_nn(wk, mk)
            w[o:e, o:e] = wk
            rows = w.at[pl.ds(o, NB), :]
            remote(rows, rows, w_send.at[k], w_recv.at[k], partner).start()
            if k < 3:
                wait_row(k + 1)
                for j in range(k + 1):
                    rest = block(k + 1, j)
                    for i in range(j):
                        rest = rest - dot_nt(low[k + 1, i], low[j, i])
                    if j == k:
                        low[k + 1, "left"] = rest
                    else:
                        low[k + 1, j] = dot_nt(rest, inv[j])

        @pl.loop(0, n_c)
        def _(i):
            per = n_c // 6
            for q in range(4):
                rows = pl.ds(pl.multiple_of(q * (TILE // 4) + i % per * CCH, CCH), CCH)
                for src_row in range(2):
                    dst = pct.at[src_row, i // per, rows, :]
                    remote(dst, dst, b_send.at[0], c_core.at[src_row, q, i], partner).wait_recv()
        @pl.loop(0, n_r)
        def _(i):
            per = n_r // 3
            rows = pl.ds(pl.multiple_of(i % per * CCH, CCH), CCH)
            for c in range(2):
                dst = rp.at[c, i // per, rows, :]
                remote(dst, dst, b_send.at[0], r_core.at[c, i], partner).wait_recv()
        slot = 0
        for cond, kids in trees:
            @pl.when(cond)
            def _():
                for n, kid in enumerate(kids):
                    remote(first, first, b_send.at[slot + n], b_recv, kid).wait_send()
            slot += len(kids)
        for k in range(4):
            rows = w.at[pl.ds(k * NB, NB), :]
            remote(rows, rows, w_send.at[k], w_recv.at[k], partner).wait_send()

    copies = [
        pltpu.make_async_copy(pct, pct_out, out_sem.at[0]),
        pltpu.make_async_copy(rp.at[:, :, pl.ds(core * NB, NB), :], rp_out, out_sem.at[1]),
        pltpu.make_async_copy(w, w_out, out_sem.at[2]),
    ]
    for copy in copies:
        copy.start()
    for copy in copies:
        copy.wait()


def gather(cov):
    dma = pltpu.SemaphoreType.DMA
    n_c = TILE // 4 // CCH * 6
    n_r = NB // CCH * 3
    return pl.pallas_call(
        gather_kernel,
        out_shape=(
            jax.ShapeDtypeStruct((2, 6, TILE, TILE), F32),
            jax.ShapeDtypeStruct((2, 3, NB, TILE), F32),
            jax.ShapeDtypeStruct((PANEL, PANEL), F32),
        ),
        in_specs=[pl.BlockSpec(memory_space=pl.ANY)],
        out_specs=[pl.BlockSpec(memory_space=pl.ANY)] * 3,
        scratch_shapes=[
            pltpu.VMEM((2, 6, TILE, TILE), F32),
            pltpu.VMEM((2, 3, TILE, TILE), F32),
            pltpu.VMEM((PANEL, PANEL), F32),
            pltpu.VMEM((PANEL, PANEL), F32),
            dma, dma((9,)), dma((2, 4, n_c)), dma((2, 2, n_r)), dma((4,)),
            dma((9,)), dma((2, 4, n_c)), dma((2, n_r)),
            dma((13,)), dma((9, 6)), dma((2, 4, 2)), dma((2, 2)), dma((3, 9)), dma((4,)), dma((3,)),
        ],
        compiler_params=pltpu.CompilerParams(collective_id=0, has_side_effects=True),
        name="gather_and_factor",
    )(cov)


def update_kernel(where, cov, pct, rp, w, out, c_all, t_hi, t_lo):
    b = pl.program_id(0)
    row, z, core = where[0], where[1], where[2]
    nt, nn = ((1,), (1,)), ((1,), (0,))

    @pl.when(b == 0)
    def _():
        wsplit = split(w[...])
        rows = jnp.concatenate([rp[c].reshape(3 * NB, TILE) for c in range(2)], axis=1)
        c = dot3(split(rows), wsplit, nt)
        c_all[...] = c
        hi, lo = split(dot3(split(c), wsplit, nn))
        t_hi[...] = hi
        t_lo[...] = lo

    cols = jnp.concatenate([pct[0, 0], pct[1, 0]], axis=0)
    old = cov[:, 0, 0, 0].reshape(3 * NB, TILE)
    new = old - dot3((t_hi[...], t_lo[...]), split(cols), nn)
    sub = lax.broadcasted_iota(jnp.int32, (3 * NB, TILE), 0)
    lane = lax.broadcasted_iota(jnp.int32, (3 * NB, TILE), 1)
    top = (sub < NB) & (row < 2)
    out[...] = jnp.where(top, 0.0, new).reshape(3, 1, 1, 1, NB, TILE)

    @pl.when((b == 0) & (z < 2))
    def _():
        mine = jnp.where(z == 0, c_all[:, :TILE], c_all[:, TILE:])
        above = top & (row * TILE + core * NB + sub < z * TILE + lane)
        out[...] = jnp.where(above, 0.0, mine).reshape(3, 1, 1, 1, NB, TILE)


def update(where, cov, pct, rp, w):
    grid_spec = pltpu.PrefetchScalarGridSpec(
        num_scalar_prefetch=1,
        grid=(6,),
        in_specs=[
            pl.BlockSpec((3, 1, 1, 1, NB, TILE), lambda b, p: (0, 0, b, 0, p[2], 0)),
            pl.BlockSpec((2, 1, TILE, TILE), lambda b, p: (0, b, 0, 0)),
            pl.BlockSpec((2, 3, NB, TILE), lambda b, p: (0, 0, 0, 0)),
            pl.BlockSpec((PANEL, PANEL), lambda b, p: (0, 0)),
        ],
        out_specs=pl.BlockSpec((3, 1, 1, 1, NB, TILE), lambda b, p: (0, 0, b, 0, 0, 0)),
        scratch_shapes=[
            pltpu.VMEM((3 * NB, PANEL), F32),
            pltpu.VMEM((3 * NB, PANEL), BF16),
            pltpu.VMEM((3 * NB, PANEL), BF16),
        ],
    )
    return pl.pallas_call(
        update_kernel,
        out_shape=jax.ShapeDtypeStruct((3, 1, 6, 1, NB, TILE), F32),
        grid_spec=grid_spec,
        name="update",
    )(where, cov, pct, rp, w)


def on_device(covariance):
    where = jnp.stack([lax.axis_index("row"), lax.axis_index("col"), lax.axis_index("depth")])
    pct, rp, w = gather(covariance)
    return update(where, covariance, pct, rp, w)


def solution(mesh):
    return jax.shard_map(
        on_device,
        mesh=mesh,
        in_specs=(P(None, "row", None, "col", None, None),),
        out_specs=P(None, "row", None, "col", "depth", None),
        check_vma=False,
    )
```

time: 631 us -> 65.9 us (0.10)
  the two profiles are of different devices: /device:TPU:83 before, /device:TPU:1 now
where the time goes in v1:
time: 65.9 us; the launch traced here: 65.6 us
  Pallas kernels  65 us (99%)
    pallas_call x1, Pallas kernels, gather(): pl.pallas_call(gather_kernel, out_shape=(jax.ShapeDtypeStruct((2, 6, TILE...  55.5 us
    pallas_call x1, Pallas kernels, update(): pl.pallas_call(update_kernel, out_shape=jax.ShapeDtypeStruct((3, 1, 6, 1,...  9.5 us

profile of v1, /device:TPU:1, one launch (start us, length us, event | category | flops | bytes accessed | tf_op | source)
XLA Modules:
  0.0 65.6 jit_solution(13588493657340820724)
XLA Ops:
  0.0 0.6 pad_add_fusion.where
  0.6 55.5 %gather_and_factor.1 = (f32[2,6,256,256]{3,2,1,0:T(8,128)}, f32[2,3,128,256]{3,2,1,0:T(8,128)}, f32[512,512]{1,0:T(8,128)}) custom-call(f32[3,1,6,1,256,256]{5,4,3,2,1,0:T(8,128)} %cov.3), custom_call_target="tpu_custom_call" | custom-call | tf_op jit(solution)/shard_map/gather_and_factor/pallas_call | solution.py:372
  56.1 9.5 %update.1 = f32[3,1,6,1,128,256]{5,4,3,2,1,0:T(8,128)} custom-call(s32[3]{0:T(128)} %pad_add_fusion.where, f32[3,1,6,1,256,256]{5,4,3,2,1,0:T(8,128)} %cov.3, f32[2,6,256,256]{3,2,1,0:T(8,128)} %get-tuple-element.8.pct, f32[2,3,128,256]{3,2,1,0:T(8,128)} %get-tuple-element.9.rp, f32[512,512]{1,0:T(8,128)} %get-tuple-element.10.w), custom_call_target="tpu_custom_call" | custom-call | tf_op jit(solution)/shard_map/update/pallas_call | solution.py:442

commit v2 on v1

v2 whole, which is shorter than its diff:
```python
import functools

import jax
import jax.numpy as jnp
from jax import lax
from jax.experimental import pallas as pl
from jax.experimental.pallas import tpu as pltpu
from jax.sharding import PartitionSpec as P

TILE = 256
PANEL = 512
NB = 128
NX = NY = 4
NZ = 8
CCH = 32
LAG = 2
TURNS = 6 * (TILE // 4 // CCH) + LAG * 7
HALF = TILE // 2
MESH = pl.DeviceIdType.MESH
HIGHEST = lax.Precision.HIGHEST
F32 = jnp.float32
BF16 = jnp.bfloat16


def dot_nt(a, b):
    dims = (((1,), (1,)), ((), ()))
    return lax.dot_general(a, b, dims, precision=HIGHEST, preferred_element_type=F32)


def dot_nn(a, b):
    dims = (((1,), (0,)), ((), ()))
    return lax.dot_general(a, b, dims, precision=HIGHEST, preferred_element_type=F32)


def split(x):
    hi = x.astype(BF16)
    return hi, (x - hi.astype(F32)).astype(BF16)


def dot3(a, b, dims):
    (ah, al), (bh, bl) = a, b
    dot = functools.partial(lax.dot_general, dimension_numbers=(dims, ((), ())), preferred_element_type=F32)
    return dot(ah, bh) + (dot(ah, bl) + dot(al, bh))


def lane_copy(v, k):
    return jnp.broadcast_to(v[:, k : k + 1], (8, NB))


def row_copy(v, k):
    return jnp.broadcast_to(v[k : k + 1, :], (8, NB))


def inverse_factor(rows):
    rows = list(rows)
    lane = lax.broadcasted_iota(jnp.int32, (8, NB), 1)
    sub = lax.broadcasted_iota(jnp.int32, (8, NB), 0)
    out = []
    for b in range(16):
        base = 8 * b
        cols = [[lane_copy(rows[i], base + k) for k in range(8)] for i in range(b, 16)]
        inside = (lane >= base) & (lane < base + 8)
        cur = jnp.where(inside, jnp.where(lane == sub + base, 1.0, 0.0), rows[b])
        diag = cols[0]
        scaled = jnp.zeros((8, NB), F32)
        for k in range(8):
            d = row_copy(diag[k], k)
            r = 1.0 / d
            scaled = jnp.where(sub == k, cur * lax.rsqrt(d), scaled)
            less = jnp.where(sub == k, diag[k] - 1.0, diag[k])
            for j in range(k + 1, 8):
                diag[j] = diag[j] - less * (row_copy(diag[k], j) * r)
            cur = cur - less * (row_copy(cur, k) * r)
        for i in range(b + 1, 16):
            acc = jnp.where(inside, 0.0, rows[i])
            for j in range(8):
                acc = acc - cols[i - b][j] * row_copy(cur, j)
            rows[i] = acc
        out.append(jnp.where(lane < base + 8, scaled, 0.0))
    return out


def panel_kernel(
    cov, out, pct, rp, s, w, m3, mine, c_all, t_hi, t_lo,
    b_recv, d_recv, c_recv, r_recv, p_recv, d_core, c_core, r_core, p_core,
    b_send, d_send, c_send, r_send, k_send, p_send, in_sem, out_sem,
):
    row = lax.axis_index("row")
    z = lax.axis_index("col")
    core = lax.axis_index("depth")
    x, y = row // NY, row % NY

    def at(xx, yy, zz, cc):
        return {"row": lax.rem(xx + NX, NX) * NY + lax.rem(yy + NY, NY), "col": lax.rem(zz + NZ, NZ), "depth": cc}

    def remote(src, dst, send, recv, to):
        return pltpu.make_async_remote_copy(src, dst, send, recv, device_id=to, device_id_type=MESH)

    partner = {"row": row, "col": z, "depth": 1 - core}
    links = [
        at(x + 1, y, z, 1), at(x - 1, y, z, 1), at(x, y + 1, z, 1),
        at(x, y - 1, z, 1), at(x, y, z + 1, 1), at(x, y, z - 1, 1),
    ]
    z_kids = [at(x, y, z + n, 0) for n in (4, 5, 3, 6, 2, 7, 1)]
    y_kids = [at(x, y + n, z, 0) for n in (2, 1, 3)]
    x_kids = [at(x + n, y, z, 0) for n in (2, 1, 3)]
    hub = row == 0
    trees = [(hub & (z == 0), z_kids), (hub, y_kids), (x == 0, x_kids)]

    own = [
        pltpu.make_async_copy(cov.at[:, 0, b, 0, pl.ds(core * HALF, HALF), :], mine.at[:, b], in_sem.at[b])
        for b in range(6)
    ]

    barrier = pltpu.get_barrier_semaphore()
    pl.semaphore_signal(barrier, inc=1, device_id=partner, device_id_type=MESH)

    @pl.when(core == 1)
    def _():
        for link in links:
            pl.semaphore_signal(barrier, inc=1, device_id=link, device_id_type=MESH)
        pl.semaphore_wait(barrier, 7)

    @pl.when(core == 0)
    def _():
        @pl.when(x != 0)
        def _():
            pl.semaphore_signal(barrier, inc=1, device_id=at(0 * x, y, z, 0), device_id_type=MESH)
        @pl.when((x == 0) & (y != 0))
        def _():
            pl.semaphore_signal(barrier, inc=1, device_id=at(x, 0 * y, z, 0), device_id_type=MESH)
        @pl.when(hub & (z != 0))
        def _():
            pl.semaphore_signal(barrier, inc=1, device_id=at(x, y, 0 * z, 0), device_id_type=MESH)
        pl.semaphore_wait(barrier, 1 + sum(cond.astype(jnp.int32) * len(kids) for cond, kids in trees))

    blocks = [(i, j) for i in range(1, 4) for j in range(i + 1)]

    def d_place(n):
        i, j = blocks[n]
        return s.at[pl.ds(i * NB, NB), pl.ds(j * NB, NB)]

    def d_tree(n):
        i, j = blocks[n]
        src_row, src_z = i // 2, j // 2
        dz = lax.rem(z - src_z + NZ, NZ)
        kids = [(4, hub & (dz <= 3)), (5, hub & ((dz == 0) | (dz >= 6)))]
        hops = jnp.minimum(dz, NZ - dz) + jnp.where(hub, src_row, 0)
        here = (row == src_row) & (dz == 0)
        if src_row:
            kids.append((3, here))
        return kids, hub | here, here, hops

    def c_tree(src, q):
        dx, dy = x, lax.rem(y - src + NY, NY)
        if q % 2:
            dx, dy = lax.rem(NX - dx, NX), lax.rem(NY - dy, NY)
        if q >= 2:
            dx, dy = dy, dx
        along = (dy == 0) & (dx <= 2) | (dx == 3) & (dy >= 1)
        across = (dx >= 1) & (dy <= 2)
        hops = jnp.where((dx == 0) & (dy > 0), dy + 4, dx + dy)
        one, two = (q % 2, 2 + q % 2) if q < 2 else (2 + q % 2, q % 2)
        return [(one, along), (two, across)], hops

    def r_tree(c, way):
        hops = lax.rem((z - c if way == 0 else c - z) + NZ, NZ)
        return [(4 + way, hops <= 6)], hops

    def pass_on(live, src, dst, here, kids, sends, recv, to_core):
        def forward(ref):
            for n, (link, cond) in enumerate(kids):
                @pl.when(cond)
                def _():
                    remote(ref, dst, sends(n), recv, links[link]).start()
            to_core(ref)

        @pl.when(live & here)
        def _():
            forward(src)

        @pl.when(live & jnp.logical_not(here))
        def _():
            remote(dst, dst, sends(0), recv, partner).wait_recv()
            forward(dst)

    n_c = TILE // 4 // CCH * 6
    n_r = NB // CCH * 3

    def piece(k):
        if k == 3:
            return m3
        i = min(k, 3)
        return w.at[pl.ds(i * NB, NB), pl.ds(0, (i + 1) * NB)] if k < 3 else w.at[pl.ds(3 * NB, NB), pl.ds(3 * NB, NB)]

    def hand_out(k):
        slot = 0
        for cond, kids in trees[1:]:
            @pl.when(cond)
            def _():
                for n, kid in enumerate(kids):
                    remote(piece(k), piece(k), p_send.at[k, slot + n], p_recv.at[k], kid).start()
            slot += len(kids)
        remote(piece(k), piece(k), p_send.at[k, slot], p_core.at[k], partner).start()

    @pl.when(core == 1)
    def _():
        @pl.loop(0, TURNS)
        def _(g):
            for n, (bi, bj) in enumerate(blocks):
                kids, on_way, here, hops = d_tree(n)
                src = cov.at[0, 0, 0, 0, pl.ds(bi % 2 * NB, NB), pl.ds(bj % 2 * NB, NB)]
                dst = d_place(n)
                def to_core(ref):
                    @pl.when(hub)
                    def _():
                        remote(ref, dst, k_send.at[0, n], d_core.at[n], partner).start()
                pass_on(on_way & (g == n // 2 + LAG * hops), src, dst, here, kids, lambda m: d_send.at[n, m], d_recv.at[n], to_core)
            for q in range(4):
                for src_row in range(2):
                    kids, hops = c_tree(src_row, q)
                    i = g - LAG * hops
                    live = (i >= 0) & (i < n_c)
                    i = jnp.clip(i, 0, n_c - 1)
                    per = n_c // 6
                    b = i // per
                    rows = pl.ds(pl.multiple_of(q * (TILE // 4) + i % per * CCH, CCH), CCH)
                    src = cov.at[0, 0, b, 0, rows, :]
                    dst = pct.at[src_row, b, rows, :]
                    def to_core(ref):
                        remote(ref, dst, k_send.at[1, src_row * 4 + q], c_core.at[src_row, q, i], partner).start()
                    pass_on(live, src, dst, hops == 0, kids, lambda m: c_send.at[src_row, q, m], c_recv.at[src_row, q, i], to_core)
            for way in range(2):
                for c in range(2):
                    kids, hops = r_tree(c, way)
                    i = g - LAG * hops
                    live = (i >= 0) & (i < n_r)
                    i = jnp.clip(i, 0, n_r - 1)
                    per = n_r // 3
                    a = i // per
                    rows = pl.ds(pl.multiple_of(way * NB + i % per * CCH, CCH), CCH)
                    src = cov.at[a, 0, 0, 0, rows, :]
                    dst = rp.at[c, a, rows, :]
                    def to_core(ref):
                        if way == 0:
                            remote(ref, dst, k_send.at[2, c], r_core.at[c, i], partner).start()
                    pass_on(live, src, dst, hops == 0, kids, lambda m: r_send.at[c, way], r_recv.at[c, way, i], to_core)

        @pl.when((x == 0) & (y <= 1))
        def _():
            copy = pltpu.make_async_copy(cov.at[0, 0, :, 0], pct.at[y], out_sem.at[0])
            copy.start()
            copy.wait()
        @pl.when(z <= 1)
        def _():
            copy = pltpu.make_async_copy(cov.at[:, 0, 0, 0], rp.at[z], out_sem.at[0])
            copy.start()
            copy.wait()
        for copy in own:
            copy.start()
        for k in range(5):
            remote(piece(k), piece(k), p_send.at[0, 0], p_core.at[k], partner).wait_recv()

    @pl.when((core == 0) & jnp.logical_not(hub))
    def _():
        for copy in own:
            copy.start()
        for k in range(5):
            remote(piece(k), piece(k), p_send.at[0, 0], p_recv.at[k], partner).wait_recv()
            hand_out(k)

    @pl.when((core == 0) & hub)
    def _():
        first = s.at[pl.ds(0, NB), pl.ds(0, NB)]
        first_in = cov.at[0, 0, 0, 0, pl.ds(0, NB), pl.ds(0, NB)]

        @pl.when(z == 0)
        def _():
            for n, kid in enumerate(z_kids):
                remote(first_in, first, b_send.at[n], b_recv, kid).start()
            copy = pltpu.make_async_copy(first_in, first, out_sem.at[0])
            copy.start()
            copy.wait()
        @pl.when(z != 0)
        def _():
            remote(first, first, b_send.at[0], b_recv, partner).wait_recv()

        def block(i, j):
            return s[i * NB : (i + 1) * NB, j * NB : (j + 1) * NB]

        def wait_row(i):
            for n, at_n in enumerate(blocks):
                if at_n[0] == i:
                    remote(d_place(n), d_place(n), b_send.at[0], d_core.at[n], partner).wait_recv()

        low = {}
        inv = {}
        for k in range(4):
            o = k * NB
            piv = block(k, k)
            if k > 0:
                low[k, k - 1] = dot_nt(low.pop((k, "left")), inv[k - 1])
                for j in range(k):
                    piv = piv - dot_nt(low[k, j], low[k, j])
                mk = None
                for j in range(k):
                    part = dot_nn(low[k, j], w[j * NB : (j + 1) * NB, : (j + 1) * NB])
                    if j < k - 1:
                        part = jnp.concatenate([part, jnp.zeros((NB, (k - 1 - j) * NB), F32)], axis=1)
                    mk = part if mk is None else mk + part
                if k == 3:
                    m3[...] = mk
                    hand_out(3)
            wk = jnp.concatenate(inverse_factor([piv[8 * i : 8 * i + 8] for i in range(16)]), axis=0)
            inv[k] = wk
            if 0 < k < 3:
                w[o : o + NB, :o] = -dot_nn(wk, mk)
            w[o : o + NB, o : o + NB] = wk
            hand_out(k if k < 3 else 4)
            if k == 0:
                for copy in own:
                    copy.start()
            if k < 3:
                wait_row(k + 1)
                for j in range(k + 1):
                    rest = block(k + 1, j)
                    for i in range(j):
                        rest = rest - dot_nt(low[k + 1, i], low[j, i])
                    if j == k:
                        low[k + 1, "left"] = rest
                    else:
                        low[k + 1, j] = dot_nt(rest, inv[j])

    @pl.when(core == 0)
    def _():
        @pl.loop(0, n_c)
        def _(i):
            per = n_c // 6
            for q in range(4):
                rows = pl.ds(pl.multiple_of(q * (TILE // 4) + i % per * CCH, CCH), CCH)
                for src_row in range(2):
                    dst = pct.at[src_row, i // per, rows, :]
                    remote(dst, dst, b_send.at[0], c_core.at[src_row, q, i], partner).wait_recv()
        @pl.loop(0, n_r)
        def _(i):
            per = n_r // 3
            rows = pl.ds(pl.multiple_of(i % per * CCH, CCH), CCH)
            for c in range(2):
                dst = rp.at[c, i // per, rows, :]
                remote(dst, dst, b_send.at[0], r_core.at[c, i], partner).wait_recv()

    parts = lambda ref: split(ref)
    tri = [parts(w[j * NB : (j + 1) * NB, : (j + 1) * NB]) for j in range(3)]
    last = w[3 * NB :, 3 * NB :]
    left = dot_nn(last, m3[...])
    tri.append(parts(jnp.concatenate([-left, last], axis=1)))
    nt, nn = ((1,), (1,)), ((1,), (0,))
    rows = [rp[c, :, pl.ds(core * HALF, HALF), :].reshape(3 * HALF, TILE) for c in range(2)]
    r_hi, r_lo = split(jnp.concatenate(rows, axis=1))
    c_parts = []
    for j in range(4):
        e = (j + 1) * NB
        got = dot3((r_hi[:, :e], r_lo[:, :e]), tri[j], nt)
        c_all[:, j * NB : e] = got
        c_parts.append(split(got))
    for j in range(4):
        cols = slice(j * NB, (j + 1) * NB)
        lhs = [jnp.concatenate([c_parts[i][h] for i in range(j, 4)], axis=1) for h in range(2)]
        rhs = [jnp.concatenate([tri[i][h][:, cols] for i in range(j, 4)], axis=0) for h in range(2)]
        hi, lo = split(dot3(lhs, rhs, nn))
        t_hi[:, cols] = hi
        t_lo[:, cols] = lo

    sub = lax.broadcasted_iota(jnp.int32, (3 * HALF, TILE), 0)
    lane = lax.broadcasted_iota(jnp.int32, (3 * HALF, TILE), 1)
    top = (sub < HALF) & (row < 2)

    def put(b):
        return pltpu.make_async_copy(mine.at[:, b], out.at[:, 0, b, 0], out_sem.at[b])

    for copy in own:
        copy.wait()

    @pl.loop(0, 6)
    def _(b):
        cols = jnp.concatenate([pct[0, b], pct[1, b]], axis=0)
        old = mine[:, b].reshape(3 * HALF, TILE)
        new = old - dot3((t_hi[...], t_lo[...]), split(cols), nn)
        mine[:, b] = jnp.where(top, 0.0, new).reshape(3, HALF, TILE)

        @pl.when((b == 0) & (z < 2))
        def _():
            panel = jnp.where(z == 0, c_all[:, :TILE], c_all[:, TILE:])
            above = top & (row * TILE + core * HALF + sub < z * TILE + lane)
            mine[:, 0] = jnp.where(above, 0.0, panel).reshape(3, HALF, TILE)
        put(b).start()

    def left_for(whole, send):
        remote(whole, whole, send, p_recv.at[0], partner).wait_send()

    @pl.when(core == 1)
    def _():
        for n in range(len(blocks)):
            kids, _, _, _ = d_tree(n)
            for m, (_, cond) in enumerate(kids):
                @pl.when(cond)
                def _():
                    left_for(d_place(n), d_send.at[n, m])
            @pl.when(hub)
            def _():
                left_for(d_place(n), k_send.at[0, n])
        for src_row in range(2):
            for q in range(4):
                kids, _ = c_tree(src_row, q)
                whole = pct.at[src_row, :, pl.ds(q * (TILE // 4), TILE // 4), :]
                for m, (_, cond) in enumerate(kids):
                    @pl.when(cond)
                    def _():
                        left_for(whole, c_send.at[src_row, q, m])
                left_for(whole, k_send.at[1, src_row * 4 + q])
        for c in range(2):
            for way in range(2):
                kids, _ = r_tree(c, way)
                whole = rp.at[c, :, pl.ds(way * NB, NB), :]
                @pl.when(kids[0][1])
                def _():
                    left_for(whole, r_send.at[c, way])
                if way == 0:
                    left_for(whole, k_send.at[2, c])

    @pl.when(core == 0)
    def _():
        first = s.at[pl.ds(0, NB), pl.ds(0, NB)]
        @pl.when(trees[0][0])
        def _():
            for n in range(len(z_kids)):
                left_for(first, b_send.at[n])
        for k in range(5):
            slot = 0
            for cond, kids in trees[1:]:
                @pl.when(cond)
                def _():
                    for n in range(len(kids)):
                        left_for(piece(k), p_send.at[k, slot + n])
                slot += len(kids)
            left_for(piece(k), p_send.at[k, slot])

    @pl.loop(0, 6)
    def _(b):
        put(b).wait()


def on_device(covariance):
    dma = pltpu.SemaphoreType.DMA
    n_c = TILE // 4 // CCH * 6
    n_r = NB // CCH * 3
    return pl.pallas_call(
        panel_kernel,
        out_shape=jax.ShapeDtypeStruct((3, 1, 6, 1, HALF, TILE), F32),
        in_specs=[pl.BlockSpec(memory_space=pl.ANY)],
        out_specs=pl.BlockSpec(memory_space=pl.ANY),
        scratch_shapes=[
            pltpu.VMEM((2, 6, TILE, TILE), F32),
            pltpu.VMEM((2, 3, TILE, TILE), F32),
            pltpu.VMEM((PANEL, PANEL), F32),
            pltpu.VMEM((PANEL, PANEL), F32),
            pltpu.VMEM((NB, 3 * NB), F32),
            pltpu.VMEM((3, 6, HALF, TILE), F32),
            pltpu.VMEM((3 * HALF, PANEL), F32),
            pltpu.VMEM((3 * HALF, PANEL), BF16),
            pltpu.VMEM((3 * HALF, PANEL), BF16),
            dma, dma((9,)), dma((2, 4, n_c)), dma((2, 2, n_r)), dma((5,)),
            dma((9,)), dma((2, 4, n_c)), dma((2, n_r)), dma((5,)),
            dma((7,)), dma((9, 3)), dma((2, 4, 2)), dma((2, 2)), dma((3, 9)), dma((5, 7)), dma((6,)), dma((6,)),
        ],
        compiler_params=pltpu.CompilerParams(collective_id=0, has_side_effects=True),
        name="panel_step",
    )(covariance)


def solution(mesh):
    return jax.shard_map(
        on_device,
        mesh=mesh,
        in_specs=(P(None, "row", None, "col", None, None),),
        out_specs=P(None, "row", None, "col", "depth", None),
        check_vma=False,
    )
```

time: 65.9 us -> 62.8 us (0.953)
  the two profiles are of different devices: /device:TPU:1 before, /device:TPU:43 now
where the time goes in v2:
time: 62.8 us; the launch traced here: 62.6 us
  Pallas kernels  59.3 us (94%)
  local copies, waits for them, and re-layouts  3.27 us (5%)
    pallas_call x1, Pallas kernels, on_device(): pl.pallas_call(panel_kernel, out_shape=jax.ShapeDtypeStruct((3, 1, 6, 1,...  59.3 us
    unnamed x1, local copies, waits for them, and re-layouts  3.27 us

profile of v2, /device:TPU:43, one launch (start us, length us, event | category | flops | bytes accessed | tf_op | source)
XLA Modules:
  0.0 62.6 jit_solution(720795921109745302)
XLA Ops:
  0.0 59.3 %panel_step.1 = f32[3,1,6,1,128,256]{5,4,3,2,1,0:T(8,128)} custom-call(f32[3,1,6,1,256,256]{5,4,3,2,1,0:T(8,128)} %cov.1), custom_call_target="tpu_custom_call" | custom-call | tf_op jit(solution)/shard_map/panel_step/pallas_call | solution.py:457
  59.3 3.3 %copy.3 = f32[3,1,6,1,128,256]{5,4,3,2,1,0:T(8,128)} copy(f32[3,1,6,1,128,256]{5,4,3,2,1,0:T(8,128)} %panel_step.1) | data formatting | bytes 4718592

commit v3 on v2

--- a/solution.py
+++ b/solution.py
@@ -12,7 +12,7 @@
 NB = 128
 NX = NY = 4
 NZ = 8
-CCH = 32
+CCH = 64
 LAG = 2
 TURNS = 6 * (TILE // 4 // CCH) + LAG * 7
 HALF = TILE // 2
@@ -81,9 +81,9 @@
 
 
 def panel_kernel(
-    cov, out, pct, rp, s, w, m3, mine, c_all, t_hi, t_lo,
-    b_recv, d_recv, c_recv, r_recv, p_recv, d_core, c_core, r_core, p_core,
-    b_send, d_send, c_send, r_send, k_send, p_send, in_sem, out_sem,
+    cov, out, pct, rp, s, w, mine, c_all, t_hi, t_lo,
+    b_recv, d_recv, a_recv, c_recv, r_recv, p_recv, c_core, r_core, p_core,
+    b_send, a_send, c_send, r_send, k_send, p_send, in_sem, out_sem, local_sem,
 ):
     row = lax.axis_index("row")
     z = lax.axis_index("col")
@@ -108,9 +108,32 @@
     trees = [(hub & (z == 0), z_kids), (hub, y_kids), (x == 0, x_kids)]
 
     own = [
-        pltpu.make_async_copy(cov.at[:, 0, b, 0, pl.ds(core * HALF, HALF), :], mine.at[:, b], in_sem.at[b])
+        pltpu.make_async_copy(cov.at[:, 0, b, 0, pl.ds(core * HALF, HALF), :], mine.at[:, b], in_sem)
         for b in range(6)
     ]
+
+    blocks = [
+        (1, 0, 1, 0), (1, 1, 3, 0), (2, 0, 0, 1), (2, 1, 1, 1), (2, 2, 0, 1),
+        (3, 0, 3, 1), (3, 1, 0, 2), (3, 2, 1, 1), (3, 3, 3, 1),
+    ]
+
+    def d_place(n):
+        i, j, _, _ = blocks[n]
+        return s.at[pl.ds(i * NB, NB), pl.ds(j * NB, NB)]
+
+    def d_input(n):
+        i, j, _, _ = blocks[n]
+        return cov.at[0, 0, 0, 0, pl.ds(i % 2 * NB, NB), pl.ds(j % 2 * NB, NB)]
+
+    def d_roles(n):
+        i, j, ax, ay = blocks[n]
+        source = (x == 0) & (y == i // 2) & (z == j // 2)
+        agent = (x == ax) & (y == ay) & (z == j // 2)
+        return source, agent, (ax, ay) == (0, i // 2)
+
+    hubs = [at(0 * x, 0 * y, n + 0 * z, 0) for n in (4, 5, 3, 6, 2, 7, 1, 0)]
+    outs = [[n for n in range(9) if blocks[n][0] // 2 == sy and blocks[n][1] // 2 == sz and not d_roles(n)[2]] for sy, sz in ((0, 0), (1, 0), (1, 1))]
+    d_rows = {1: s.at[pl.ds(0, NB), pl.ds(0, 2 * NB)], 2: s.at[pl.ds(0, NB), pl.ds(0, 3 * NB)], 3: s.at[pl.ds(0, NB), :]}
 
     barrier = pltpu.get_barrier_semaphore()
     pl.semaphore_signal(barrier, inc=1, device_id=partner, device_id_type=MESH)
@@ -132,24 +155,42 @@
         @pl.when(hub & (z != 0))
         def _():
             pl.semaphore_signal(barrier, inc=1, device_id=at(x, y, 0 * z, 0), device_id_type=MESH)
-        pl.semaphore_wait(barrier, 1 + sum(cond.astype(jnp.int32) * len(kids) for cond, kids in trees))
-
-    blocks = [(i, j) for i in range(1, 4) for j in range(i + 1)]
-
-    def d_place(n):
-        i, j = blocks[n]
-        return s.at[pl.ds(i * NB, NB), pl.ds(j * NB, NB)]
-
-    def d_tree(n):
-        i, j = blocks[n]
-        src_row, src_z = i // 2, j // 2
-        dz = lax.rem(z - src_z + NZ, NZ)
-        kids = [(4, hub & (dz <= 3)), (5, hub & ((dz == 0) | (dz >= 6)))]
-        hops = jnp.minimum(dz, NZ - dz) + jnp.where(hub, src_row, 0)
-        here = (row == src_row) & (dz == 0)
-        if src_row:
-            kids.append((3, here))
-        return kids, hub | here, here, hops
+        want = 1 + sum(cond.astype(jnp.int32) * len(kids) for cond, kids in trees)
+        for n in range(9):
+            i, j, ax, ay = blocks[n]
+            source, agent, same = d_roles(n)
+            @pl.when(hub)
+            def _():
+                to = at(0 * x + ax, 0 * y + ay, 0 * z + j // 2, 0)
+                pl.semaphore_signal(barrier, inc=1, device_id=to, device_id_type=MESH)
+            want += agent.astype(jnp.int32) * 8
+            if not same:
+                @pl.when(agent)
+                def _():
+                    to = at(0 * x, 0 * y + i // 2, z, 0)
+                    pl.semaphore_signal(barrier, inc=1, device_id=to, device_id_type=MESH)
+                want += source.astype(jnp.int32)
+        pl.semaphore_wait(barrier, want)
+
+    @pl.when(core == 0)
+    def _():
+        for n in range(9):
+            i, j, ax, ay = blocks[n]
+            source, agent, same = d_roles(n)
+            if not same:
+                @pl.when(source)
+                def _():
+                    to = at(0 * x + ax, 0 * y + ay, z, 0)
+                    remote(d_input(n), d_place(n), a_send.at[0], a_recv, to).start()
+        for n in range(9):
+            i, j, ax, ay = blocks[n]
+            source, agent, same = d_roles(n)
+            @pl.when(agent)
+            def _():
+                if not same:
+                    remote(d_place(n), d_place(n), a_send.at[0], a_recv, partner).wait_recv()
+                for to in hubs:
+                    remote(d_input(n) if same else d_place(n), d_place(n), a_send.at[1], d_recv.at[i - 1], to).start()
 
     def c_tree(src, q):
         dx, dy = x, lax.rem(y - src + NY, NY)
@@ -187,11 +228,14 @@
     n_c = TILE // 4 // CCH * 6
     n_r = NB // CCH * 3
 
+    pieces = [(0, 0), (1, 0), (2, 0), (1, 1), (2, 1), (3, 0), (3, 1), (2, 2), (3, 2), (3, 3)]
+
     def piece(k):
-        if k == 3:
-            return m3
-        i = min(k, 3)
-        return w.at[pl.ds(i * NB, NB), pl.ds(0, (i + 1) * NB)] if k < 3 else w.at[pl.ds(3 * NB, NB), pl.ds(3 * NB, NB)]
+        i, j = pieces[k]
+        return w.at[pl.ds(i * NB, NB), pl.ds(j * NB, NB)]
+
+    def piece_value(i, j):
+        return w[i * NB : (i + 1) * NB, j * NB : (j + 1) * NB]
 
     def hand_out(k):
         slot = 0
@@ -199,23 +243,14 @@
             @pl.when(cond)
             def _():
                 for n, kid in enumerate(kids):
-                    remote(piece(k), piece(k), p_send.at[k, slot + n], p_recv.at[k], kid).start()
+                    remote(piece(k), piece(k), p_send.at[slot + n], p_recv.at[k], kid).start()
             slot += len(kids)
-        remote(piece(k), piece(k), p_send.at[k, slot], p_core.at[k], partner).start()
+        remote(piece(k), piece(k), p_send.at[slot], p_core.at[k], partner).start()
 
     @pl.when(core == 1)
     def _():
         @pl.loop(0, TURNS)
         def _(g):
-            for n, (bi, bj) in enumerate(blocks):
-                kids, on_way, here, hops = d_tree(n)
-                src = cov.at[0, 0, 0, 0, pl.ds(bi % 2 * NB, NB), pl.ds(bj % 2 * NB, NB)]
-                dst = d_place(n)
-                def to_core(ref):
-                    @pl.when(hub)
-                    def _():
-                        remote(ref, dst, k_send.at[0, n], d_core.at[n], partner).start()
-                pass_on(on_way & (g == n // 2 + LAG * hops), src, dst, here, kids, lambda m: d_send.at[n, m], d_recv.at[n], to_core)
             for q in range(4):
                 for src_row in range(2):
                     kids, hops = c_tree(src_row, q)
@@ -228,7 +263,17 @@
                     src = cov.at[0, 0, b, 0, rows, :]
                     dst = pct.at[src_row, b, rows, :]
                     def to_core(ref):
-                        remote(ref, dst, k_send.at[1, src_row * 4 + q], c_core.at[src_row, q, i], partner).start()
+                        for h in range(2):
+                            @pl.when(i == n_c // 2 * (h + 1) - 1)
+                            def _():
+                                part = pl.ds(3 * h, 3), 0, pl.ds(q * (TILE // 4), TILE // 4)
+                                home = pct.at[src_row, part[0], part[2], :]
+                                @pl.when(hops == 0)
+                                def _():
+                                    remote(cov.at[0, 0, part[0], 0, part[2], :], home, k_send.at[0], c_core.at[src_row, q, h], partner).start()
+                                @pl.when(hops != 0)
+                                def _():
+                                    remote(home, home, k_send.at[0], c_core.at[src_row, q, h], partner).start()
                     pass_on(live, src, dst, hops == 0, kids, lambda m: c_send.at[src_row, q, m], c_recv.at[src_row, q, i], to_core)
             for way in range(2):
                 for c in range(2):
@@ -243,30 +288,38 @@
                     dst = rp.at[c, a, rows, :]
                     def to_core(ref):
                         if way == 0:
-                            remote(ref, dst, k_send.at[2, c], r_core.at[c, i], partner).start()
+                            @pl.when(i % (n_r // 3) == n_r // 3 - 1)
+                            def _():
+                                home = rp.at[c, a, pl.ds(0, NB), :]
+                                @pl.when(hops == 0)
+                                def _():
+                                    remote(cov.at[a, 0, 0, 0, pl.ds(0, NB), :], home, k_send.at[1], r_core.at[c, a], partner).start()
+                                @pl.when(hops != 0)
+                                def _():
+                                    remote(home, home, k_send.at[1], r_core.at[c, a], partner).start()
                     pass_on(live, src, dst, hops == 0, kids, lambda m: r_send.at[c, way], r_recv.at[c, way, i], to_core)
 
         @pl.when((x == 0) & (y <= 1))
         def _():
-            copy = pltpu.make_async_copy(cov.at[0, 0, :, 0], pct.at[y], out_sem.at[0])
+            copy = pltpu.make_async_copy(cov.at[0, 0, :, 0], pct.at[y], local_sem)
             copy.start()
             copy.wait()
         @pl.when(z <= 1)
         def _():
-            copy = pltpu.make_async_copy(cov.at[:, 0, 0, 0], rp.at[z], out_sem.at[0])
+            copy = pltpu.make_async_copy(cov.at[:, 0, 0, 0], rp.at[z], local_sem)
             copy.start()
             copy.wait()
         for copy in own:
             copy.start()
-        for k in range(5):
-            remote(piece(k), piece(k), p_send.at[0, 0], p_core.at[k], partner).wait_recv()
+        for k in range(len(pieces)):
+            remote(piece(k), piece(k), p_send.at[0], p_core.at[k], partner).wait_recv()
 
     @pl.when((core == 0) & jnp.logical_not(hub))
     def _():
         for copy in own:
             copy.start()
-        for k in range(5):
-            remote(piece(k), piece(k), p_send.at[0, 0], p_recv.at[k], partner).wait_recv()
+        for k in range(len(pieces)):
+            remote(piece(k), piece(k), p_send.at[0], p_recv.at[k], partner).wait_recv()
             hand_out(k)
 
     @pl.when((core == 0) & hub)
@@ -278,7 +331,7 @@
         def _():
             for n, kid in enumerate(z_kids):
                 remote(first_in, first, b_send.at[n], b_recv, kid).start()
-            copy = pltpu.make_async_copy(first_in, first, out_sem.at[0])
+            copy = pltpu.make_async_copy(first_in, first, local_sem)
             copy.start()
             copy.wait()
         @pl.when(z != 0)
@@ -289,71 +342,68 @@
             return s[i * NB : (i + 1) * NB, j * NB : (j + 1) * NB]
 
         def wait_row(i):
-            for n, at_n in enumerate(blocks):
-                if at_n[0] == i:
-                    remote(d_place(n), d_place(n), b_send.at[0], d_core.at[n], partner).wait_recv()
+            remote(d_rows[i], d_rows[i], b_send.at[0], d_recv.at[i - 1], partner).wait_recv()
 
         low = {}
         inv = {}
+
+        def publish(i, j, value):
+            w[i * NB : (i + 1) * NB, j * NB : (j + 1) * NB] = value
+            hand_out(pieces.index((i, j)))
+
+        def solve(i, j):
+            rest = block(i, j)
+            for n in range(j):
+                rest = rest - dot_nt(low[i, n], low[j, n])
+            low[i, j] = dot_nt(rest, inv[j])
+            publish(i, j, low[i, j])
+
         for k in range(4):
-            o = k * NB
+            if k == 1:
+                wait_row(1)
+            if k > 0:
+                solve(k, k - 1)
             piv = block(k, k)
-            if k > 0:
-                low[k, k - 1] = dot_nt(low.pop((k, "left")), inv[k - 1])
+            for j in range(k):
+                piv = piv - dot_nt(low[k, j], low[k, j])
+            if 0 < k < 3:
+                wait_row(k + 1)
                 for j in range(k):
-                    piv = piv - dot_nt(low[k, j], low[k, j])
-                mk = None
-                for j in range(k):
-                    part = dot_nn(low[k, j], w[j * NB : (j + 1) * NB, : (j + 1) * NB])
-                    if j < k - 1:
-                        part = jnp.concatenate([part, jnp.zeros((NB, (k - 1 - j) * NB), F32)], axis=1)
-                    mk = part if mk is None else mk + part
-                if k == 3:
-                    m3[...] = mk
-                    hand_out(3)
-            wk = jnp.concatenate(inverse_factor([piv[8 * i : 8 * i + 8] for i in range(16)]), axis=0)
-            inv[k] = wk
-            if 0 < k < 3:
-                w[o : o + NB, :o] = -dot_nn(wk, mk)
-            w[o : o + NB, o : o + NB] = wk
-            hand_out(k if k < 3 else 4)
+                    solve(k + 1, j)
+            inv[k] = jnp.concatenate(inverse_factor([piv[8 * i : 8 * i + 8] for i in range(16)]), axis=0)
+            publish(k, k, inv[k])
             if k == 0:
                 for copy in own:
                     copy.start()
-            if k < 3:
-                wait_row(k + 1)
-                for j in range(k + 1):
-                    rest = block(k + 1, j)
-                    for i in range(j):
-                        rest = rest - dot_nt(low[k + 1, i], low[j, i])
-                    if j == k:
-                        low[k + 1, "left"] = rest
-                    else:
-                        low[k + 1, j] = dot_nt(rest, inv[j])
 
     @pl.when(core == 0)
     def _():
-        @pl.loop(0, n_c)
-        def _(i):
-            per = n_c // 6
-            for q in range(4):
-                rows = pl.ds(pl.multiple_of(q * (TILE // 4) + i % per * CCH, CCH), CCH)
-                for src_row in range(2):
-                    dst = pct.at[src_row, i // per, rows, :]
-                    remote(dst, dst, b_send.at[0], c_core.at[src_row, q, i], partner).wait_recv()
-        @pl.loop(0, n_r)
-        def _(i):
-            per = n_r // 3
-            rows = pl.ds(pl.multiple_of(i % per * CCH, CCH), CCH)
-            for c in range(2):
-                dst = rp.at[c, i // per, rows, :]
-                remote(dst, dst, b_send.at[0], r_core.at[c, i], partner).wait_recv()
-
-    parts = lambda ref: split(ref)
-    tri = [parts(w[j * NB : (j + 1) * NB, : (j + 1) * NB]) for j in range(3)]
-    last = w[3 * NB :, 3 * NB :]
-    left = dot_nn(last, m3[...])
-    tri.append(parts(jnp.concatenate([-left, last], axis=1)))
+        for q in range(4):
+            for src_row in range(2):
+                for h in range(2):
+                    dst = pct.at[src_row, pl.ds(3 * h, 3), pl.ds(q * (TILE // 4), TILE // 4), :]
+                    remote(dst, dst, b_send.at[0], c_core.at[src_row, q, h], partner).wait_recv()
+        for c in range(2):
+            for a in range(3):
+                dst = rp.at[c, a, pl.ds(0, NB), :]
+                remote(dst, dst, b_send.at[0], r_core.at[c, a], partner).wait_recv()
+
+    inverse_rows = []
+    for i in range(4):
+        diag = piece_value(i, i)
+        row_blocks = []
+        for j in range(i):
+            acc = None
+            for n in range(j, i):
+                part = dot_nn(piece_value(i, n), inverse_rows[n][:, j * NB : (j + 1) * NB])
+                acc = part if acc is None else acc + part
+            row_blocks.append(acc)
+        if i == 0:
+            inverse_rows.append(diag)
+        else:
+            left = -dot_nn(diag, jnp.concatenate(row_blocks, axis=1))
+            inverse_rows.append(jnp.concatenate([left, diag], axis=1))
+    tri = [split(v) for v in inverse_rows]
     nt, nn = ((1,), (1,)), ((1,), (0,))
     rows = [rp[c, :, pl.ds(core * HALF, HALF), :].reshape(3 * HALF, TILE) for c in range(2)]
     r_hi, r_lo = split(jnp.concatenate(rows, axis=1))
@@ -376,10 +426,9 @@
     top = (sub < HALF) & (row < 2)
 
     def put(b):
-        return pltpu.make_async_copy(mine.at[:, b], out.at[:, 0, b, 0], out_sem.at[b])
-
-    for copy in own:
-        copy.wait()
+        return pltpu.make_async_copy(mine.at[:, b], out.at[:, 0, b, 0], out_sem)
+
+    pltpu.make_async_copy(mine, mine, in_sem).wait()
 
     @pl.loop(0, 6)
     def _(b):
@@ -396,19 +445,10 @@
         put(b).start()
 
     def left_for(whole, send):
-        remote(whole, whole, send, p_recv.at[0], partner).wait_send()
+        remote(whole, whole, send, b_recv, partner).wait_send()
 
     @pl.when(core == 1)
     def _():
-        for n in range(len(blocks)):
-            kids, _, _, _ = d_tree(n)
-            for m, (_, cond) in enumerate(kids):
-                @pl.when(cond)
-                def _():
-                    left_for(d_place(n), d_send.at[n, m])
-            @pl.when(hub)
-            def _():
-                left_for(d_place(n), k_send.at[0, n])
         for src_row in range(2):
             for q in range(4):
                 kids, _ = c_tree(src_row, q)
@@ -417,37 +457,40 @@
                     @pl.when(cond)
                     def _():
                         left_for(whole, c_send.at[src_row, q, m])
-                left_for(whole, k_send.at[1, src_row * 4 + q])
         for c in range(2):
             for way in range(2):
                 kids, _ = r_tree(c, way)
-                whole = rp.at[c, :, pl.ds(way * NB, NB), :]
                 @pl.when(kids[0][1])
                 def _():
-                    left_for(whole, r_send.at[c, way])
-                if way == 0:
-                    left_for(whole, k_send.at[2, c])
+                    left_for(rp.at[c, :, pl.ds(way * NB, NB), :], r_send.at[c, way])
+        left_for(pct, k_send.at[0])
+        left_for(rp.at[:, :, pl.ds(0, NB), :], k_send.at[1])
 
     @pl.when(core == 0)
     def _():
-        first = s.at[pl.ds(0, NB), pl.ds(0, NB)]
         @pl.when(trees[0][0])
         def _():
             for n in range(len(z_kids)):
-                left_for(first, b_send.at[n])
-        for k in range(5):
-            slot = 0
-            for cond, kids in trees[1:]:
-                @pl.when(cond)
-                def _():
-                    for n in range(len(kids)):
-                        left_for(piece(k), p_send.at[k, slot + n])
-                slot += len(kids)
-            left_for(piece(k), p_send.at[k, slot])
-
-    @pl.loop(0, 6)
-    def _(b):
-        put(b).wait()
+                left_for(s.at[pl.ds(0, NB), pl.ds(0, NB)], b_send.at[n])
+        for group, (sy, sz) in zip(outs, ((0, 0), (1, 0), (1, 1))):
+            @pl.when((x == 0) & (y == sy) & (z == sz))
+            def _():
+                left_for(s.at[pl.ds(0, NB), pl.ds(0, len(group) * NB)], a_send.at[0])
+        for n in range(9):
+            @pl.when(d_roles(n)[1])
+            def _():
+                left_for(s.at[pl.ds(0, 2 * NB), :], a_send.at[1])
+        all_pieces = pct.at[0, pl.ds(0, 5), pl.ds(0, NB), :]
+        slot = 0
+        for cond, kids in trees[1:]:
+            @pl.when(cond)
+            def _():
+                for n in range(len(kids)):
+                    left_for(all_pieces, p_send.at[slot + n])
+            slot += len(kids)
+        left_for(all_pieces, p_send.at[slot])
+
+    pltpu.make_async_copy(mine, mine, out_sem).wait()
 
 
 def on_device(covariance):
@@ -464,14 +507,12 @@
             pltpu.VMEM((2, 3, TILE, TILE), F32),
             pltpu.VMEM((PANEL, PANEL), F32),
             pltpu.VMEM((PANEL, PANEL), F32),
-            pltpu.VMEM((NB, 3 * NB), F32),
             pltpu.VMEM((3, 6, HALF, TILE), F32),
             pltpu.VMEM((3 * HALF, PANEL), F32),
             pltpu.VMEM((3 * HALF, PANEL), BF16),
             pltpu.VMEM((3 * HALF, PANEL), BF16),
-            dma, dma((9,)), dma((2, 4, n_c)), dma((2, 2, n_r)), dma((5,)),
-            dma((9,)), dma((2, 4, n_c)), dma((2, n_r)), dma((5,)),
-            dma((7,)), dma((9, 3)), dma((2, 4, 2)), dma((2, 2)), dma((3, 9)), dma((5, 7)), dma((6,)), dma((6,)),
+            dma, dma((3,)), dma, dma((2, 4, n_c)), dma((2, 2, n_r)), dma((10,)), dma((2, 4, 2)), dma((2, 3)), dma((10,)),
+            dma((7,)), dma((2,)), dma((2, 4, 2)), dma((2, 2)), dma((2,)), dma((7,)), dma, dma, dma,
         ],
         compiler_params=pltpu.CompilerParams(collective_id=0, has_side_effects=True),
         name="panel_step",

time: 62.8 us -> 56.2 us (0.89)
  Pallas kernels: 59.3 us -> 52.7 us
    pallas_call x1, Pallas kernels: 59.3 us -> 52.7 us  [on_device(): pl.pallas_call(panel_kernel, out_shape=jax.ShapeDtypeStruct((3, 1, 6, 1,...]
where the time goes in v3:
time: 56.2 us; the launch traced here: 56 us
  Pallas kernels  52.7 us (94%)
  local copies, waits for them, and re-layouts  3.27 us (6%)
    pallas_call x1, Pallas kernels, on_device(): pl.pallas_call(panel_kernel, out_shape=jax.ShapeDtypeStruct((3, 1, 6, 1,...  52.7 us
    unnamed x1, local copies, waits for them, and re-layouts  3.27 us

profile of v3, /device:TPU:43, one launch (start us, length us, event | category | flops | bytes accessed | tf_op | source)
XLA Modules:
  0.0 56.0 jit_solution(9030890059949058810)
XLA Ops:
  0.0 52.7 %panel_step.1 = f32[3,1,6,1,128,256]{5,4,3,2,1,0:T(8,128)} custom-call(f32[3,1,6,1,256,256]{5,4,3,2,1,0:T(8,128)} %cov.1), custom_call_target="tpu_custom_call" | custom-call | tf_op jit(solution)/shard_map/panel_step/pallas_call | solution.py:500
  52.7 3.3 %copy.3 = f32[3,1,6,1,128,256]{5,4,3,2,1,0:T(8,128)} copy(f32[3,1,6,1,128,256]{5,4,3,2,1,0:T(8,128)} %panel_step.1) | data formatting | bytes 4718592

commit v4 on v3

--- a/solution.py
+++ b/solution.py
@@ -81,7 +81,7 @@
 
 
 def panel_kernel(
-    cov, out, pct, rp, s, w, mine, c_all, t_hi, t_lo,
+    cov, out, pct, rp, s, w, mine, c_all, t_all, m3, t_hi, t_lo, p_hi, p_lo,
     b_recv, d_recv, a_recv, c_recv, r_recv, p_recv, c_core, r_core, p_core,
     b_send, a_send, c_send, r_send, k_send, p_send, in_sem, out_sem, local_sem,
 ):
@@ -246,6 +246,16 @@
                     remote(piece(k), piece(k), p_send.at[slot + n], p_recv.at[k], kid).start()
             slot += len(kids)
         remote(piece(k), piece(k), p_send.at[slot], p_core.at[k], partner).start()
+
+    def take(k):
+        @pl.when(core == 1)
+        def _():
+            remote(piece(k), piece(k), p_send.at[0], p_core.at[k], partner).wait_recv()
+
+        @pl.when((core == 0) & jnp.logical_not(hub))
+        def _():
+            remote(piece(k), piece(k), p_send.at[0], p_recv.at[k], partner).wait_recv()
+            hand_out(k)
 
     @pl.when(core == 1)
     def _():
@@ -311,16 +321,11 @@
             copy.wait()
         for copy in own:
             copy.start()
-        for k in range(len(pieces)):
-            remote(piece(k), piece(k), p_send.at[0], p_core.at[k], partner).wait_recv()
 
     @pl.when((core == 0) & jnp.logical_not(hub))
     def _():
         for copy in own:
             copy.start()
-        for k in range(len(pieces)):
-            remote(piece(k), piece(k), p_send.at[0], p_recv.at[k], partner).wait_recv()
-            hand_out(k)
 
     @pl.when((core == 0) & hub)
     def _():
@@ -351,12 +356,16 @@
             w[i * NB : (i + 1) * NB, j * NB : (j + 1) * NB] = value
             hand_out(pieces.index((i, j)))
 
+        def product(a, b):
+            return dot3(a, b, ((1,), (1,)))
+
         def solve(i, j):
             rest = block(i, j)
             for n in range(j):
-                rest = rest - dot_nt(low[i, n], low[j, n])
-            low[i, j] = dot_nt(rest, inv[j])
-            publish(i, j, low[i, j])
+                rest = rest - product(low[i, n], low[j, n])
+            got = product(split(rest), inv[j])
+            low[i, j] = split(got)
+            publish(i, j, got)
 
         for k in range(4):
             if k == 1:
@@ -365,16 +374,49 @@
                 solve(k, k - 1)
             piv = block(k, k)
             for j in range(k):
-                piv = piv - dot_nt(low[k, j], low[k, j])
+                piv = piv - product(low[k, j], low[k, j])
             if 0 < k < 3:
                 wait_row(k + 1)
                 for j in range(k):
                     solve(k + 1, j)
-            inv[k] = jnp.concatenate(inverse_factor([piv[8 * i : 8 * i + 8] for i in range(16)]), axis=0)
-            publish(k, k, inv[k])
+            wk = jnp.concatenate(inverse_factor([piv[8 * i : 8 * i + 8] for i in range(16)]), axis=0)
+            publish(k, k, wk)
+            inv[k] = split(wk)
             if k == 0:
                 for copy in own:
                     copy.start()
+
+    late = len(pieces) - 2
+    last = len(pieces) - 1
+    for k in range(late):
+        take(k)
+    nt, nn = ((1,), (1,)), ((1,), (0,))
+
+    inverse_rows = []
+    for i in range(4):
+        if i == 3:
+            take(late)
+        row_blocks = []
+        for j in range(i):
+            acc = None
+            for n in range(j, i):
+                part = dot_nn(piece_value(i, n), inverse_rows[n][:, j * NB : (j + 1) * NB])
+                acc = part if acc is None else acc + part
+            row_blocks.append(acc)
+        if i == 0:
+            inverse_rows.append(piece_value(0, 0))
+        elif i < 3:
+            left = -dot_nn(piece_value(i, i), jnp.concatenate(row_blocks, axis=1))
+            inverse_rows.append(jnp.concatenate([left, piece_value(i, i)], axis=1))
+        else:
+            m3[...] = jnp.concatenate(row_blocks, axis=1)
+    tri = [split(v) for v in inverse_rows]
+
+    passes_on = (core == 0) & (x == 0)
+
+    @pl.when(passes_on)
+    def _():
+        take(last)
 
     @pl.when(core == 0)
     def _():
@@ -388,38 +430,42 @@
                 dst = rp.at[c, a, pl.ds(0, NB), :]
                 remote(dst, dst, b_send.at[0], r_core.at[c, a], partner).wait_recv()
 
-    inverse_rows = []
-    for i in range(4):
-        diag = piece_value(i, i)
-        row_blocks = []
-        for j in range(i):
-            acc = None
-            for n in range(j, i):
-                part = dot_nn(piece_value(i, n), inverse_rows[n][:, j * NB : (j + 1) * NB])
-                acc = part if acc is None else acc + part
-            row_blocks.append(acc)
-        if i == 0:
-            inverse_rows.append(diag)
-        else:
-            left = -dot_nn(diag, jnp.concatenate(row_blocks, axis=1))
-            inverse_rows.append(jnp.concatenate([left, diag], axis=1))
-    tri = [split(v) for v in inverse_rows]
-    nt, nn = ((1,), (1,)), ((1,), (0,))
     rows = [rp[c, :, pl.ds(core * HALF, HALF), :].reshape(3 * HALF, TILE) for c in range(2)]
     r_hi, r_lo = split(jnp.concatenate(rows, axis=1))
     c_parts = []
-    for j in range(4):
+    for j in range(3):
         e = (j + 1) * NB
         got = dot3((r_hi[:, :e], r_lo[:, :e]), tri[j], nt)
         c_all[:, j * NB : e] = got
         c_parts.append(split(got))
-    for j in range(4):
+    for j in range(3):
         cols = slice(j * NB, (j + 1) * NB)
-        lhs = [jnp.concatenate([c_parts[i][h] for i in range(j, 4)], axis=1) for h in range(2)]
-        rhs = [jnp.concatenate([tri[i][h][:, cols] for i in range(j, 4)], axis=0) for h in range(2)]
-        hi, lo = split(dot3(lhs, rhs, nn))
-        t_hi[:, cols] = hi
-        t_lo[:, cols] = lo
+        lhs = [jnp.concatenate([c_parts[i][h] for i in range(j, 3)], axis=1) for h in range(2)]
+        rhs = [jnp.concatenate([tri[i][h][:, cols] for i in range(j, 3)], axis=0) for h in range(2)]
+        t_all[:, cols] = dot3(lhs, rhs, nn)
+
+    @pl.loop(0, 6)
+    def _(b):
+        for c in range(2):
+            hi, lo = split(pct[c, b])
+            p_hi[b, c * TILE : (c + 1) * TILE] = hi
+            p_lo[b, c * TILE : (c + 1) * TILE] = lo
+
+    @pl.when(jnp.logical_not(passes_on))
+    def _():
+        take(last)
+
+    left = -dot_nn(piece_value(3, 3), m3[...])
+    end = split(jnp.concatenate([left, piece_value(3, 3)], axis=1))
+    c_last = dot3((r_hi, r_lo), end, nt)
+    c_all[:, 3 * NB :] = c_last
+    t_last = dot3(split(c_last), end, nn)
+    hi, lo = split(t_all[...] + t_last[:, : 3 * NB])
+    t_hi[:, : 3 * NB] = hi
+    t_lo[:, : 3 * NB] = lo
+    hi, lo = split(t_last[:, 3 * NB :])
+    t_hi[:, 3 * NB :] = hi
+    t_lo[:, 3 * NB :] = lo
 
     sub = lax.broadcasted_iota(jnp.int32, (3 * HALF, TILE), 0)
     lane = lax.broadcasted_iota(jnp.int32, (3 * HALF, TILE), 1)
@@ -432,9 +478,8 @@
 
     @pl.loop(0, 6)
     def _(b):
-        cols = jnp.concatenate([pct[0, b], pct[1, b]], axis=0)
         old = mine[:, b].reshape(3 * HALF, TILE)
-        new = old - dot3((t_hi[...], t_lo[...]), split(cols), nn)
+        new = old - dot3((t_hi[...], t_lo[...]), (p_hi[b], p_lo[b]), nn)
         mine[:, b] = jnp.where(top, 0.0, new).reshape(3, HALF, TILE)
 
         @pl.when((b == 0) & (z < 2))
@@ -500,7 +545,7 @@
     return pl.pallas_call(
         panel_kernel,
         out_shape=jax.ShapeDtypeStruct((3, 1, 6, 1, HALF, TILE), F32),
-        in_specs=[pl.BlockSpec(memory_space=pl.ANY)],
+        in_specs=[pl.BlockSpec(memory_space=pltpu.HBM)],
         out_specs=pl.BlockSpec(memory_space=pl.ANY),
         scratch_shapes=[
             pltpu.VMEM((2, 6, TILE, TILE), F32),
@@ -509,12 +554,16 @@
             pltpu.VMEM((PANEL, PANEL), F32),
             pltpu.VMEM((3, 6, HALF, TILE), F32),
             pltpu.VMEM((3 * HALF, PANEL), F32),
+            pltpu.VMEM((3 * HALF, 3 * NB), F32),
+            pltpu.VMEM((NB, 3 * NB), F32),
             pltpu.VMEM((3 * HALF, PANEL), BF16),
             pltpu.VMEM((3 * HALF, PANEL), BF16),
+            pltpu.VMEM((6, PANEL, TILE), BF16),
+            pltpu.VMEM((6, PANEL, TILE), BF16),
             dma, dma((3,)), dma, dma((2, 4, n_c)), dma((2, 2, n_r)), dma((10,)), dma((2, 4, 2)), dma((2, 3)), dma((10,)),
             dma((7,)), dma((2,)), dma((2, 4, 2)), dma((2, 2)), dma((2,)), dma((7,)), dma, dma, dma,
         ],
-        compiler_params=pltpu.CompilerParams(collective_id=0, has_side_effects=True),
+        compiler_params=pltpu.CompilerParams(collective_id=0, has_side_effects=True, vmem_limit_bytes=48 * 1024 * 1024),
         name="panel_step",
     )(covariance)
 

time: 56.2 us -> 53 us (0.943)
  the two profiles are of different devices: /device:TPU:43 before, /device:TPU:1 now
where the time goes in v4:
time: 53 us; the launch traced here: 52.9 us
  Pallas kernels  51.5 us (97%)
  local copies, waits for them, and re-layouts  1.41 us (3%)
    pallas_call x1, Pallas kernels, on_device(): pl.pallas_call(panel_kernel, out_shape=jax.ShapeDtypeStruct((3, 1, 6, 1,...  51.5 us
    unnamed x1, local copies, waits for them, and re-layouts  1.41 us

profile of v4, /device:TPU:1, one launch (start us, length us, event | category | flops | bytes accessed | tf_op | source)
XLA Modules:
  0.0 52.9 jit_solution(2819016189606516109)
XLA Ops:
  0.0 51.5 %panel_step.1 = f32[3,1,6,1,128,256]{5,4,3,2,1,0:T(8,128)S(1)} custom-call(f32[3,1,6,1,256,256]{5,4,3,2,1,0:T(8,128)} %cov.1), custom_call_target="tpu_custom_call" | custom-call | tf_op jit(solution)/shard_map/panel_step/pallas_call | solution.py:545
  51.5 1.4 %copy.3 = f32[3,1,6,1,128,256]{5,4,3,2,1,0:T(8,128)} copy(f32[3,1,6,1,128,256]{5,4,3,2,1,0:T(8,128)S(1)} %panel_step.1) | data formatting | bytes 4718592

commit v5 on v4

--- a/solution.py
+++ b/solution.py
@@ -13,7 +13,7 @@
 NX = NY = 4
 NZ = 8
 CCH = 64
-LAG = 2
+LAG = 3
 TURNS = 6 * (TILE // 4 // CCH) + LAG * 7
 HALF = TILE // 2
 MESH = pl.DeviceIdType.MESH
@@ -83,7 +83,7 @@
 def panel_kernel(
     cov, out, pct, rp, s, w, mine, c_all, t_all, m3, t_hi, t_lo, p_hi, p_lo,
     b_recv, d_recv, a_recv, c_recv, r_recv, p_recv, c_core, r_core, p_core,
-    b_send, a_send, c_send, r_send, k_send, p_send, in_sem, out_sem, local_sem,
+    b_send, a_send, c_send, r_send, k_send, p_send, in_sem, out_sem, local_sem, rows_sem, cols_sem,
 ):
     row = lax.axis_index("row")
     z = lax.axis_index("col")
@@ -256,6 +256,19 @@
         def _():
             remote(piece(k), piece(k), p_send.at[0], p_recv.at[k], partner).wait_recv()
             hand_out(k)
+
+    own_rows = (x == 0) & (y <= 1) & (core == 1)
+    own_cols = (z <= 1) & (core == 1)
+
+    @pl.when(own_rows)
+    def _():
+        for b in range(6):
+            pltpu.make_async_copy(cov.at[0, 0, b, 0], pct.at[y, b], rows_sem).start()
+
+    @pl.when(own_cols)
+    def _():
+        for a in range(3):
+            pltpu.make_async_copy(cov.at[a, 0, 0, 0], rp.at[z, a], cols_sem).start()
 
     @pl.when(core == 1)
     def _():
@@ -309,16 +322,6 @@
                                     remote(home, home, k_send.at[1], r_core.at[c, a], partner).start()
                     pass_on(live, src, dst, hops == 0, kids, lambda m: r_send.at[c, way], r_recv.at[c, way, i], to_core)
 
-        @pl.when((x == 0) & (y <= 1))
-        def _():
-            copy = pltpu.make_async_copy(cov.at[0, 0, :, 0], pct.at[y], local_sem)
-            copy.start()
-            copy.wait()
-        @pl.when(z <= 1)
-        def _():
-            copy = pltpu.make_async_copy(cov.at[:, 0, 0, 0], rp.at[z], local_sem)
-            copy.start()
-            copy.wait()
         for copy in own:
             copy.start()
 
@@ -429,6 +432,14 @@
             for a in range(3):
                 dst = rp.at[c, a, pl.ds(0, NB), :]
                 remote(dst, dst, b_send.at[0], r_core.at[c, a], partner).wait_recv()
+
+    @pl.when(own_rows)
+    def _():
+        pltpu.make_async_copy(pct.at[y], pct.at[y], rows_sem).wait()
+
+    @pl.when(own_cols)
+    def _():
+        pltpu.make_async_copy(rp.at[z], rp.at[z], cols_sem).wait()
 
     rows = [rp[c, :, pl.ds(core * HALF, HALF), :].reshape(3 * HALF, TILE) for c in range(2)]
     r_hi, r_lo = split(jnp.concatenate(rows, axis=1))
@@ -561,7 +572,7 @@
             pltpu.VMEM((6, PANEL, TILE), BF16),
             pltpu.VMEM((6, PANEL, TILE), BF16),
             dma, dma((3,)), dma, dma((2, 4, n_c)), dma((2, 2, n_r)), dma((10,)), dma((2, 4, 2)), dma((2, 3)), dma((10,)),
-            dma((7,)), dma((2,)), dma((2, 4, 2)), dma((2, 2)), dma((2,)), dma((7,)), dma, dma, dma,
+            dma((7,)), dma((2,)), dma((2, 4, 2)), dma((2, 2)), dma((2,)), dma((7,)), dma, dma, dma, dma, dma,
         ],
         compiler_params=pltpu.CompilerParams(collective_id=0, has_side_effects=True, vmem_limit_bytes=48 * 1024 * 1024),
         name="panel_step",

time: 53 us -> 50.2 us (0.947)
  the two profiles are of different devices: /device:TPU:1 before, /device:TPU:43 now
where the time goes in v5:
time: 50.2 us; the launch traced here: 50 us
  Pallas kernels  48.6 us (97%)
  local copies, waits for them, and re-layouts  1.41 us (3%)
    pallas_call x1, Pallas kernels, on_device(): pl.pallas_call(panel_kernel, out_shape=jax.ShapeDtypeStruct((3, 1, 6, 1,...  48.6 us
    unnamed x1, local copies, waits for them, and re-layouts  1.41 us

profile of v5, /device:TPU:43, one launch (start us, length us, event | category | flops | bytes accessed | tf_op | source)
XLA Modules:
  0.0 50.0 jit_solution(15051947492967885641)
XLA Ops:
  0.0 48.6 %panel_step.1 = f32[3,1,6,1,128,256]{5,4,3,2,1,0:T(8,128)S(1)} custom-call(f32[3,1,6,1,256,256]{5,4,3,2,1,0:T(8,128)} %cov.1), custom_call_target="tpu_custom_call" | custom-call | tf_op jit(solution)/shard_map/panel_step/pallas_call | solution.py:556
  48.6 1.4 %copy.3 = f32[3,1,6,1,128,256]{5,4,3,2,1,0:T(8,128)} copy(f32[3,1,6,1,128,256]{5,4,3,2,1,0:T(8,128)S(1)} %panel_step.1) | data formatting | bytes 4718592

commit v6 on v5

--- a/solution.py
+++ b/solution.py
@@ -17,19 +17,8 @@
 TURNS = 6 * (TILE // 4 // CCH) + LAG * 7
 HALF = TILE // 2
 MESH = pl.DeviceIdType.MESH
-HIGHEST = lax.Precision.HIGHEST
 F32 = jnp.float32
 BF16 = jnp.bfloat16
-
-
-def dot_nt(a, b):
-    dims = (((1,), (1,)), ((), ()))
-    return lax.dot_general(a, b, dims, precision=HIGHEST, preferred_element_type=F32)
-
-
-def dot_nn(a, b):
-    dims = (((1,), (0,)), ((), ()))
-    return lax.dot_general(a, b, dims, precision=HIGHEST, preferred_element_type=F32)
 
 
 def split(x):
@@ -41,6 +30,10 @@
     (ah, al), (bh, bl) = a, b
     dot = functools.partial(lax.dot_general, dimension_numbers=(dims, ((), ())), preferred_element_type=F32)
     return dot(ah, bh) + (dot(ah, bl) + dot(al, bh))
+
+
+def dot_nn(a, b):
+    return dot3(split(a), split(b), ((1,), (0,)))
 
 
 def lane_copy(v, k):

time: 50.2 us -> 50.1 us (level)
  no operation moved by 1% of the time
where the time goes in v6:
time: 50.1 us; the launch traced here: 50 us
  Pallas kernels  48.6 us (97%)
  local copies, waits for them, and re-layouts  1.41 us (3%)
    pallas_call x1, Pallas kernels, on_device(): pl.pallas_call(panel_kernel, out_shape=jax.ShapeDtypeStruct((3, 1, 6, 1,...  48.6 us
    unnamed x1, local copies, waits for them, and re-layouts  1.41 us

profile of v6, /device:TPU:43, one launch (start us, length us, event | category | flops | bytes accessed | tf_op | source)
XLA Modules:
  0.0 50.0 jit_solution(15353959765779043898)
XLA Ops:
  0.0 48.6 %panel_step.1 = f32[3,1,6,1,128,256]{5,4,3,2,1,0:T(8,128)S(1)} custom-call(f32[3,1,6,1,256,256]{5,4,3,2,1,0:T(8,128)} %cov.1), custom_call_target="tpu_custom_call" | custom-call | tf_op jit(solution)/shard_map/panel_step/pallas_call | solution.py:549
  48.6 1.4 %copy.3 = f32[3,1,6,1,128,256]{5,4,3,2,1,0:T(8,128)} copy(f32[3,1,6,1,128,256]{5,4,3,2,1,0:T(8,128)S(1)} %panel_step.1) | data formatting | bytes 4718592
